TPU v7x, 32 devices: a whole 2x2x4 slice. The times are simulated.
32 devices in a mesh: dp: 8 (over z, y), head: 4 (over x, core).
Axes of the slice: x: 2, y: 2, z: 4, core: 2. Of those that a mesh axis runs over, the one named last changes fastest.
Arguments:
- layer_input: bfloat16 [2, 16384, 768], P(None, ('dp', 'head')), may hold values from -6 to 6
- output_grad: bfloat16 [2, 16384, 768], P(None, ('dp', 'head')), may hold values from -6 to 6
- lengths: int32 [2, 32], P(None, 'dp'), may hold values from 64 to 512, as said below
- w_qkv: bfloat16 [3, 768, 768], P(None, 'dp', 'head'), may hold values from -0.21875 to 0.21875
- w_out: bfloat16 [768, 768], P('head', 'dp'), may hold values from -4 to 4
- w_up: bfloat16 [768, 3072], P('dp', 'head'), may hold values from -0.21875 to 0.21875
- w_down: bfloat16 [3072, 768], P('head', 'dp'), may hold values from -0.109375 to 0.109375
- norm_gains: float32 [2, 768], replicated, may hold values from 0.5 to 1.5
- norm_biases: float32 [2, 768], replicated, may hold values from -3 to 3
- mask_logits: float32 [12, 512, 512], P('head', 'dp'), may hold values from -9 to 9
- mask_noise: float32 [12, 512, 512], P('head', 'dp'), may hold values from -6 to 6
Outputs:
- layer_output: bfloat16 [2, 16384, 768], P(None, ('dp', 'head'))
- input_grad: float32 [2, 16384, 768], P(None, ('dp', 'head'))
- w_qkv_grad: float32 [3, 768, 768], P(None, 'dp', 'head')
- w_out_grad: float32 [768, 768], P('head', 'dp')
- w_up_grad: float32 [768, 3072], P('dp', 'head')
- w_down_grad: float32 [3072, 768], P('head', 'dp')
- gains_grad: float32 [2, 768], replicated
- biases_grad: float32 [2, 768], replicated
- logits_grad: float32 [12, 512, 512], P('head', 'dp')
Inputs may be any that keep to these rules, and one draw needn't show every extreme that they name: `lengths`: each sequence's number of valid tokens; in each micro-batch the first sequence of each index of dp has 512.
All inputs are finite; a program needn't handle non-finite values.
Results may differ from a plain program's by a relative error of at most 0.013.
The roundings to bfloat16 on the way count: a program that leaves them out, or rounds other values in their place, can miss the bound.
Values may be sent and summed in bfloat16 or wider, within the bound.
No kernel may reach another device: no remote copies, remote signals or barrier semaphores. Data moves between devices by JAX's collectives and lax.ppermute only.
A program may use at most 192 MiB of HBM per device.

v0:
```python
import math

import jax
import jax.numpy as jnp
from jax import lax
from jax.sharding import PartitionSpec as P

HEAD_DIM = 64
MICRO = 2


epsilon = 1e-05


def mat_mul(left, right):
    return jnp.dot(left, right, preferred_element_type=jnp.float32)


def inner_rows(left, right):
    return lax.dot_general(
        left, right, (((0,), (0,)), ((), ())), preferred_element_type=jnp.float32
    )


def outer_rows(left, right):
    return lax.dot_general(
        left, right, (((1,), (1,)), ((), ())), preferred_element_type=jnp.float32
    )


def widen(rows):
    return lax.all_gather(rows, "head", axis=0, tiled=True)


def narrow(partial_rows):
    return lax.psum_scatter(partial_rows, "head", scatter_dimension=0, tiled=True)


def fetch(w_qkv, w_out, w_up, w_down):
    parts = (
        lax.all_gather(w_qkv, "dp", axis=1, tiled=True),
        lax.all_gather(w_out, "dp", axis=1, tiled=True),
        lax.all_gather(w_up, "dp", axis=0, tiled=True),
        lax.all_gather(w_down, "dp", axis=1, tiled=True),
    )
    return parts


def settle(grads):
    return (
        lax.psum_scatter(grads[0], "dp", scatter_dimension=1, tiled=True),
        lax.psum_scatter(grads[1], "dp", scatter_dimension=1, tiled=True),
        lax.psum_scatter(grads[2], "dp", scatter_dimension=0, tiled=True),
        lax.psum_scatter(grads[3], "dp", scatter_dimension=1, tiled=True),
    )


def norm_forward(rows, gain, bias):
    mean = jnp.mean(rows, axis=1, keepdims=True)
    centered = rows - mean
    inverse = lax.rsqrt(jnp.mean(centered * centered, axis=1, keepdims=True) + epsilon)
    unit = centered * inverse
    return (unit * gain + bias, unit, inverse)


def norm_backward(dnormed, unit, inverse, gain):
    dgain = jnp.sum(dnormed * unit, axis=0)
    dbias = jnp.sum(dnormed, axis=0)
    dunit = dnormed * gain
    drows = inverse * (
        dunit
        - jnp.mean(dunit, axis=1, keepdims=True)
        - unit * jnp.mean(dunit * unit, axis=1, keepdims=True)
    )
    return (drows, dgain, dbias)


def attend(query, key, value, gate, size):
    scores = jnp.einsum("qhe,khe->hqk", query, key, preferred_element_type=jnp.float32) / math.sqrt(
        HEAD_DIM
    )
    key_ok = jnp.arange(scores.shape[2], dtype=jnp.int32) < size
    scores = jnp.where(key_ok[None, None, :], scores, jnp.float32(-1e30))
    top = jnp.max(scores, axis=-1, keepdims=True)
    lse = top + jnp.log(jnp.sum(jnp.exp(scores - top), axis=-1, keepdims=True))
    probs = jnp.exp(scores - lse)
    weights = (probs * gate).astype(jnp.bfloat16)
    mixed = jnp.einsum("hqk,khe->qhe", weights, value, preferred_element_type=jnp.float32)
    return (mixed.astype(jnp.bfloat16), lse)


def attend_back(query, key, value, gate, size, lse, dmixed):
    scores = jnp.einsum("qhe,khe->hqk", query, key, preferred_element_type=jnp.float32) / math.sqrt(
        HEAD_DIM
    )
    key_ok = jnp.arange(scores.shape[2], dtype=jnp.int32) < size
    probs = jnp.where(key_ok[None, None, :], jnp.exp(scores - lse), jnp.float32(0.0))
    weights = (probs * gate).astype(jnp.bfloat16)
    dweights = jnp.einsum("qhe,khe->hqk", dmixed, value, preferred_element_type=jnp.float32)
    dvalue = jnp.einsum("hqk,qhe->khe", weights, dmixed, preferred_element_type=jnp.float32)
    dgate = dweights * probs
    dprobs = dweights * gate
    dscores = probs * (dprobs - jnp.sum(dprobs * probs, axis=-1, keepdims=True))
    dscores = dscores.astype(jnp.bfloat16)
    dquery = jnp.einsum(
        "hqk,khe->qhe", dscores, key, preferred_element_type=jnp.float32
    ) / math.sqrt(HEAD_DIM)
    dkey = jnp.einsum(
        "hqk,qhe->khe", dscores, query, preferred_element_type=jnp.float32
    ) / math.sqrt(HEAD_DIM)
    return (dquery, dkey, dvalue, dgate)


def micro_step(rows, grad_rows, lens, held, gate, gains, biases):
    wqkv, wout, wup, wdown = held
    local_rows = rows.shape[0]
    count = lens.shape[0]
    span = local_rows * lax.axis_size("head")
    length = span // count
    local_width = wqkv.shape[2]
    heads = local_width // HEAD_DIM
    position = jnp.arange(length, dtype=jnp.int32)
    valid_all = (position[None, :] < lens[:, None]).reshape(span, 1)
    offset = lax.axis_index("head") * local_rows
    valid = lax.dynamic_slice_in_dim(valid_all, offset, local_rows, 0)
    full = widen(rows)
    proj = [mat_mul(full, wqkv[i]).astype(jnp.bfloat16) for i in range(3)]
    shaped = [p.reshape(count, length, heads, HEAD_DIM) for p in proj]

    def forward_seq(item):
        return attend(item[0], item[1], item[2], gate, item[3])

    mixed, lse = lax.map(forward_seq, (shaped[0], shaped[1], shaped[2], lens))
    mixed = mixed.reshape(span, local_width)
    attn = narrow(mat_mul(mixed, wout))
    first = rows.astype(jnp.float32) + attn
    normed_one, unit_one, inverse_one = norm_forward(first, gains[0], biases[0])
    hidden = normed_one.astype(jnp.bfloat16)
    hidden_full = widen(hidden)
    up = mat_mul(hidden_full, wup)
    act = jax.nn.gelu(up, approximate=False).astype(jnp.bfloat16)
    ffn = narrow(mat_mul(act, wdown))
    second = hidden.astype(jnp.float32) + ffn
    normed_two, unit_two, inverse_two = norm_forward(second, gains[1], biases[1])
    result = jnp.where(valid, normed_two, jnp.float32(0.0)).astype(jnp.bfloat16)
    dout = jnp.where(valid, grad_rows.astype(jnp.float32), jnp.float32(0.0))
    dsecond, dgain_two, dbias_two = norm_backward(dout, unit_two, inverse_two, gains[1])
    dffn_full = widen(dsecond.astype(jnp.bfloat16))
    down_grad = inner_rows(act, dffn_full)
    dact = outer_rows(dffn_full, wdown)
    unused, gelu_pull = jax.vjp(lambda value: jax.nn.gelu(value, approximate=False), up)
    dup = gelu_pull(dact)[0].astype(jnp.bfloat16)
    up_grad = inner_rows(hidden_full, dup)
    dhidden = narrow(outer_rows(dup, wup)) + dsecond
    dfirst, dgain_one, dbias_one = norm_backward(dhidden, unit_one, inverse_one, gains[0])
    dattn_full = widen(dfirst.astype(jnp.bfloat16))
    out_grad = inner_rows(mixed, dattn_full)
    dmixed = (
        outer_rows(dattn_full, wout).astype(jnp.bfloat16).reshape(count, length, heads, HEAD_DIM)
    )

    def backward_seq(carry, item):
        dquery, dkey, dvalue, dgate = attend_back(
            item[0], item[1], item[2], gate, item[3], item[4], item[5]
        )
        return (
            carry + dgate,
            (dquery.astype(jnp.bfloat16), dkey.astype(jnp.bfloat16), dvalue.astype(jnp.bfloat16)),
        )

    dgate_sum, parts = lax.scan(
        backward_seq,
        jnp.zeros(gate.shape, jnp.float32),
        (shaped[0], shaped[1], shaped[2], lens, lse, dmixed),
    )
    flat = [p.reshape(span, local_width) for p in parts]
    qkv_grad = jnp.stack([inner_rows(full, piece) for piece in flat])
    dx_part = (
        outer_rows(flat[0], wqkv[0]) + outer_rows(flat[1], wqkv[1]) + outer_rows(flat[2], wqkv[2])
    )
    dinput = narrow(dx_part) + dfirst
    norm_grads = (jnp.stack([dgain_one, dgain_two]), jnp.stack([dbias_one, dbias_two]))
    return (result, dinput, (qkv_grad, out_grad, up_grad, down_grad), norm_grads, dgate_sum)


def per_device(
    layer_input,
    output_grad,
    lengths,
    w_qkv,
    w_out,
    w_up,
    w_down,
    norm_gains,
    norm_biases,
    mask_logits,
    mask_noise,
):
    gate_part = jax.nn.sigmoid(mask_logits + mask_noise)
    gate = lax.all_gather(gate_part, "dp", axis=1, tiled=True)
    results = []
    dinputs = []
    for micro in range(MICRO):
        held = fetch(w_qkv, w_out, w_up, w_down)
        lens_here = lengths[micro]
        result, dinput, grads, norm_grads, dgate = micro_step(
            layer_input[micro], output_grad[micro], lens_here, held, gate, norm_gains, norm_biases
        )
        results.append(result)
        dinputs.append(dinput)
        if micro == 0:
            gain_total, bias_total = norm_grads
            gate_total = dgate
        else:
            gain_total = gain_total + norm_grads[0]
            bias_total = bias_total + norm_grads[1]
            gate_total = gate_total + dgate
        owned = settle(grads)
        summed = owned if micro == 0 else tuple((a + b for a, b in zip(summed, owned)))
    gain_sum, bias_sum = lax.psum((gain_total, bias_total), ("dp", "head"))
    gate_grad = lax.psum_scatter(gate_total, "dp", scatter_dimension=1, tiled=True)
    logits_grad = gate_grad * gate_part * (1.0 - gate_part)
    return (
        jnp.stack(results),
        jnp.stack(dinputs),
        summed[0],
        summed[1],
        summed[2],
        summed[3],
        gain_sum,
        bias_sum,
        logits_grad,
    )


def solution(mesh):
    placed = (
        P(None, ("dp", "head"), None),
        P(None, ("dp", "head"), None),
        P(None, "dp"),
        P(None, "dp", "head"),
        P("head", "dp"),
        P("dp", "head"),
        P("head", "dp"),
        P(),
        P(),
        P("head", "dp", None),
        P("head", "dp", None),
    )
    return jax.shard_map(
        per_device,
        mesh=mesh,
        in_specs=placed,
        out_specs=(
            P(None, ("dp", "head"), None),
            P(None, ("dp", "head"), None),
            P(None, "dp", "head"),
            P("head", "dp"),
            P("dp", "head"),
            P("head", "dp"),
            P(),
            P(),
            P("head", "dp", None),
        ),
        check_vma=False,
    )
```

profile of v0, /device:TPU:0, one launch (start us, length us, event | category | flops | bytes accessed | tf_op | source)
XLA Modules:
  0.0 1421.5 jit_solution(14790553453103822533)
XLA Ops:
  11.7 37.1 %all_gather.44 = bf16[3,768,192]{2,1,0:T(8,128)(2,1)} all-gather(bf16[3,96,192]{2,1,0:T(8,128)(2,1)S(1)} %copy-done.52), channel_id=1, replica_groups=mesh['dp'=8,'head'=4] {'dp'}, dimensions={1}, use_global_device_ids=true | all-gather | bytes 995328 | tf_op jit(solution)/shard_map/all_gather | solution.py:41
  49.0 31.8 %all_gather.46 = bf16[192,768]{0,1:T(8,128)(2,1)S(1)} all-gather(bf16[192,96]{0,1:T(8,128)(2,1)S(1)} %copy.99), channel_id=1, replica_groups=mesh['dp'=8,'head'=4] {'dp'}, dimensions={1}, use_global_device_ids=true | all-gather | bytes 331776 | tf_op jit(solution)/shard_map/all_gather | solution.py:42
  110.5 27.8 %while.59 = (s32[]{:T(128)}, bf16[4,512,3,64]{1,3,2,0:T(8,128)(2,1)}, f32[4,3,512,1]{2,1,3,0:T(4,128)}, bf16[4,512,3,64]{1,3,2,0:T(8,128)(2,1)}, s32[4]{0:T(128)...) while((s32[]{:T(128)}, ...), condition=%wide.region_13.14_spmd, body=%wide.region_10.13_spmd.sunk | while | flops 210861056 | bytes 13425261 | solution.py:133
  175.7 27.9 %while.58 = (s32[]{:T(128)}, bf16[4,512,3,64]{1,3,2,0:T(8,128)(2,1)}, f32[4,3,512,1]{2,1,3,0:T(4,128)}, bf16[4,512,3,64]{1,3,2,0:T(8,128)(2,1)}, s32[4]{0:T(128)...) while((s32[]{:T(128)}, ...), condition=%wide.region_3.4_spmd, body=%wide.region_0.3_spmd.sunk | while | flops 210861056 | bytes 13425261 | solution.py:133
  212.5 55.8 %reduce-scatter.18.cloned.1.call-done = f32[512,768]{1,0:T(8,128)} async-done(((f32[2048,768]{1,0:T(8,128)}), f32[512,768]{1,0:T(8,128)}) %reduce-scatter.18.cloned.1.call-update) | async-done | bytes 1572880 | tf_op jit(solution)/shard_map/reduce_scatter | solution.py:36
  274.5 37.0 %all-gather.18.cloned.1.call-done = bf16[768,768]{1,0:T(8,128)(2,1)} async-done(((bf16[96,768]{1,0:T(8,128)(2,1)}), bf16[768,768]{1,0:T(8,128)(2,1)}) %all-gather.18.cloned.1.call-update) | async-done | bytes 1179664 | tf_op jit(solution)/shard_map/all_gather | solution.py:43
  311.4 29.5 %all-gather.16.cloned.1.call-done = bf16[2048,768]{1,0:T(8,128)(2,1)} async-done(((bf16[512,768]{1,0:T(8,128)(2,1)}), bf16[2048,768]{1,0:T(8,128)(2,1)}) %all-gather.16.cloned.1.call-update) | async-done | bytes 3145744 | tf_op jit(solution)/shard_map/all_gather | solution.py:32
  340.9 18.5 %multiply_convert_fusion.35 = (bf16[2048,768]{1,0:T(8,128)(2,1)S(1)}, f32[2048,768]{1,0:T(8,128)}, f32[2048,768]{1,0:T(8,128)}) fusion(bf16[2048,768]{1,0:T(8,128)(2,1)} %all-gather.16.cloned.1.call-done, bf16[768,768]{1,0:T(8,128)(2,1)} %all-gather.18.cloned.1.call-done), kind=kOutput, calls=%fused_computation.145 | convolution fusion | flops 2518155264 | bytes 20054016 | tf_op jit(solution)/shard_map/dot_general | solution.py:16
  359.4 24.8 %all-gather.20.cloned.1.call-done = bf16[768,768]{0,1:T(8,128)(2,1)} async-done(((bf16[768,96]{0,1:T(8,128)(2,1)}), bf16[768,768]{0,1:T(8,128)(2,1)}) %all-gather.20.cloned.1.call-update) | async-done | bytes 1179664 | tf_op jit(solution)/shard_map/all_gather | solution.py:44
  390.1 23.0 %all-gather.22.cloned.1.call-done = bf16[2048,768]{1,0:T(8,128)(2,1)} async-done(((bf16[512,768]{1,0:T(8,128)(2,1)}), bf16[2048,768]{1,0:T(8,128)(2,1)}) %all-gather.22.cloned.1.call-update) | async-done | bytes 3145744 | tf_op jit(solution)/shard_map/all_gather | solution.py:32
  413.1 18.2 %multiply_convert_fusion.34 = (bf16[2048,768]{1,0:T(8,128)(2,1)S(1)}, f32[2048,768]{1,0:T(8,128)}, f32[2048,768]{1,0:T(8,128)}) fusion(bf16[2048,768]{1,0:T(8,128)(2,1)} %all-gather.22.cloned.1.call-done, bf16[768,768]{1,0:T(8,128)(2,1)S(1)} %copy-done.83), kind=kOutput, calls=%fused_computation.132 | convolution fusion | flops 2518155264 | bytes 20054016 | tf_op jit(solution)/shard_map/dot_general | solution.py:16
  438.5 35.3 %reduce-scatter.20.cloned.1.call-done = f32[512,768]{1,0:T(8,128)} async-done(((f32[2048,768]{1,0:T(8,128)}), f32[512,768]{1,0:T(8,128)}) %reduce-scatter.20.cloned.1.call-update) | async-done | bytes 1572880 | tf_op jit(solution)/shard_map/reduce_scatter | solution.py:36
  475.8 59.1 %reduce-scatter.24.cloned.1.call-done = f32[512,768]{1,0:T(8,128)} async-done(((f32[2048,768]{1,0:T(8,128)}), f32[512,768]{1,0:T(8,128)}) %reduce-scatter.24.cloned.1.call-update) | async-done | bytes 1572880 | tf_op jit(solution)/shard_map/reduce_scatter | solution.py:36
  542.9 27.9 %all-gather.24.cloned.1.call-done = bf16[2048,768]{1,0:T(8,128)(2,1)} async-done(((bf16[512,768]{1,0:T(8,128)(2,1)}), bf16[2048,768]{1,0:T(8,128)(2,1)}) %all-gather.24.cloned.1.call-update) | async-done | bytes 3145744 | tf_op jit(solution)/shard_map/all_gather | solution.py:32
  570.8 10.1 add_convert_fusion.1
  587.2 13.7 all-gather.28.cloned.1.call-done
  600.9 9.0 add_convert_fusion
  616.3 45.4 %reduce-scatter.26.cloned.1.call-done = f32[512,768]{1,0:T(8,128)} async-done(((f32[2048,768]{1,0:T(8,128)}), f32[512,768]{1,0:T(8,128)}) %reduce-scatter.26.cloned.1.call-update) | async-done | bytes 1572880 | tf_op jit(solution)/shard_map/reduce_scatter | solution.py:36
  667.6 55.0 %reduce-scatter.30.cloned.1.call-done = f32[512,768]{1,0:T(8,128)} async-done(((f32[2048,768]{1,0:T(8,128)}), f32[512,768]{1,0:T(8,128)}) %reduce-scatter.30.cloned.1.call-update) | async-done | bytes 1572880 | tf_op jit(solution)/shard_map/reduce_scatter | solution.py:36
  730.6 28.0 %all-gather.26.cloned.1.call-done = bf16[2048,768]{1,0:T(8,128)(2,1)} async-done(((bf16[512,768]{1,0:T(8,128)(2,1)}), bf16[2048,768]{1,0:T(8,128)(2,1)}) %all-gather.26.cloned.1.call-update) | async-done | bytes 3145744 | tf_op jit(solution)/shard_map/all_gather | solution.py:32
  771.3 74.4 %while.60 = (s32[]{:T(128)}, f32[3,512,512]{1,2,0:T(8,128)}, bf16[4,512,3,64]{1,3,2,0:T(8,128)(2,1)}, bf16[4,512,3,64]{1,3,2,0:T(8,128)(2,1)}, bf16[4,512,3,64]{...) while((s32[]{:T(128)}, f32[3,512,512]{1,2,0:T(8,128)}, ...), condition=%wide.region_27.28_spmd.clone, body=%wide.region_25.27_spmd.clone.sunk | while | flops 514817024 | bytes 41324704 | solution.py:171
  857.7 74.5 %while.61 = (s32[]{:T(128)}, f32[3,512,512]{1,2,0:T(8,128)}, bf16[4,512,3,64]{1,3,2,0:T(8,128)(2,1)}, bf16[4,512,3,64]{1,3,2,0:T(8,128)(2,1)}, bf16[4,512,3,64]{...) while((s32[]{:T(128)}, f32[3,512,512]{1,2,0:T(8,128)}, ...), condition=%wide.region_36.37_spmd.clone, body=%wide.region_34.36_spmd.clone.sunk | while | flops 514817024 | bytes 41324704 | solution.py:171
  880.9 6.2 multiply_reduce_fusion.15
  899.7 6.2 multiply_reduce_fusion.15
  918.5 6.2 multiply_reduce_fusion.15
  1005.6 40.1 %all-reduce = (f32[2,768]{1,0:T(2,128)}, f32[2,768]{1,0:T(2,128)}) all-reduce(f32[2,768]{1,0:T(2,128)S(1)} %maximum_add_fusion.1, f32[2,768]{1,0:T(2,128)S(1)} %maximum_add_fusion.2), channel_id=1, replica_groups=mesh['dp'=8,'head'=4] {'dp','head'}, use_global_device_ids=true, to_apply=%region_50.51 | all-reduce | flops 3072 | bytes 24576 | tf_op jit(solution)/shard_map/psum | solution.py:220
  1048.7 21.1 %reduce-scatter.40.cloned.1.call-done = f32[96,576]{1,0:T(8,128)} async-done(((f32[768,576]{1,0:T(8,128)}), f32[96,576]{1,0:T(8,128)}) %reduce-scatter.40.cloned.1.call-update) | async-done | bytes 221200
  1073.5 74.1 %reduce-scatter.34.cloned.1.call-done = f32[3,64,512]{2,1,0:T(8,128)} async-done(((f32[3,512,512]{2,1,0:T(8,128)}), f32[3,64,512]{2,1,0:T(8,128)}) %reduce-scatter.34.cloned.1.call-update) | async-done | bytes 393232 | tf_op jit(solution)/shard_map/reduce_scatter | solution.py:221
  1149.4 58.3 %reduce-scatter.28.cloned.1.call-done = f32[512,768]{1,0:T(8,128)} async-done(((f32[2048,768]{1,0:T(8,128)}), f32[512,768]{1,0:T(8,128)}) %reduce-scatter.28.cloned.1.call-update) | async-done | bytes 1572880 | tf_op jit(solution)/shard_map/reduce_scatter | solution.py:36
  1210.5 58.3 %reduce-scatter.32.cloned.1.call-done = f32[512,768]{1,0:T(8,128)} async-done(((f32[2048,768]{1,0:T(8,128)}), f32[512,768]{1,0:T(8,128)}) %reduce-scatter.32.cloned.1.call-update) | async-done | bytes 1572880 | tf_op jit(solution)/shard_map/reduce_scatter | solution.py:36
  1272.4 69.5 %reduce-scatter.38.cloned.1.call-done = f32[768,96]{0,1:T(8,128)} async-done(((f32[768,768]{0,1:T(8,128)}), f32[768,96]{0,1:T(8,128)}) %reduce-scatter.38.cloned.1.call-update) | async-done | bytes 294928 | tf_op jit(solution)/shard_map/reduce_scatter | solution.py:54
  1341.9 72.2 %reduce-scatter.36.cloned.1.call-done = f32[96,768]{1,0:T(8,128)} async-done(((f32[768,768]{1,0:T(8,128)}), f32[96,768]{1,0:T(8,128)}) %reduce-scatter.36.cloned.1.call-update) | async-done | bytes 294928 | tf_op jit(solution)/shard_map/reduce_scatter | solution.py:53
  (493 shorter events, 433.5 us)
Async XLA Ops:
  7.2 73.5 %all-gather.34.cloned.1.call-start = ((), (), s32[]{:S(2)}) async-start(), calls=%async_computation.32 | async-start | bytes 3932160 | tf_op jit(solution)/shard_map/all_gather | solution.py:32
  10.0 96.6 %all-gather.14.cloned.1.call-start = ((), (), s32[]{:S(2)}) async-start(), calls=%async_computation.13 | async-start | bytes 3538944 | tf_op jit(solution)/shard_map/all_gather | solution.py:200
  10.9 134.3 %all-gather.32.cloned.1.call-start = ((), (), s32[]{:S(2)}) async-start(), calls=%async_computation.31 | async-start | bytes 3932160 | tf_op jit(solution)/shard_map/all_gather | solution.py:32
  11.7 200.8 %reduce-scatter.22.cloned.1.call-start = ((), (), s32[]{:S(2)}) async-start(), calls=%async_computation.19 | async-start | bytes 7864320 | tf_op jit(solution)/shard_map/reduce_scatter | solution.py:36
  80.8 125.4 %copy-start.26 = (bf16[192,768]{0,1:T(8,128)(2,1)}, bf16[192,768]{0,1:T(8,128)(2,1)S(1)}, u32[]{:S(2)}) copy-start(bf16[192,768]{0,1:T(8,128)(2,1)S(1)} %all_gather.46) | copy-start | bytes 884740
  144.9 123.4 %reduce-scatter.18.cloned.1.call-start = ((), (), s32[]{:S(2)}) async-start(), calls=%async_computation.14 | async-start | bytes 7864320 | tf_op jit(solution)/shard_map/reduce_scatter | solution.py:36
  203.6 234.3 %copy-start.77 = (s32[4]{0:T(128)}, s32[4]{0:T(128)S(1)}, u32[]{:S(2)}) copy-start(s32[4]{0:T(128)S(1)} %get-tuple-element.1136) | copy-start | bytes 52
  210.8 100.7 %all-gather.18.cloned.1.call-start = ((), (), s32[]{:S(2)}) async-start(), calls=%async_computation.16 | async-start | bytes 1327104 | tf_op jit(solution)/shard_map/all_gather | solution.py:43
  211.3 129.6 %all-gather.16.cloned.1.call-start = ((), (), s32[]{:S(2)}) async-start(), calls=%async_computation.15 | async-start | bytes 3932160 | tf_op jit(solution)/shard_map/all_gather | solution.py:32
  272.9 111.3 %all-gather.20.cloned.1.call-start = ((), (), s32[]{:S(2)}) async-start(), calls=%async_computation.17 | async-start | bytes 1327104 | tf_op jit(solution)/shard_map/all_gather | solution.py:44
  273.7 139.4 %all-gather.22.cloned.1.call-start = ((), (), s32[]{:S(2)}) async-start(), calls=%async_computation.20 | async-start | bytes 3932160 | tf_op jit(solution)/shard_map/all_gather | solution.py:32
  274.4 199.4 %reduce-scatter.20.cloned.1.call-start = ((), (), s32[]{:S(2)}) async-start(), calls=%async_computation.18 | async-start | bytes 7864320 | tf_op jit(solution)/shard_map/reduce_scatter | solution.py:36
  390.0 144.9 %reduce-scatter.24.cloned.1.call-start = ((), (), s32[]{:S(2)}) async-start(), calls=%async_computation.21 | async-start | bytes 7864320 | tf_op jit(solution)/shard_map/reduce_scatter | solution.py:36
  437.7 133.1 %all-gather.24.cloned.1.call-start = ((), (), s32[]{:S(2)}) async-start(), calls=%async_computation.22 | async-start | bytes 3932160 | tf_op jit(solution)/shard_map/all_gather | solution.py:32
  475.5 64.0 %copy-start.11 = (f32[512,768]{1,0:T(8,128)}, f32[512,768]{1,0:T(8,128)S(1)}, u32[]{:S(2)}) copy-start(f32[512,768]{1,0:T(8,128)S(1)} %get-tuple-element.582) | copy-start | bytes 4718596
  475.8 61.3 %copy-start.13 = (bf16[2,512,768]{2,1,0:T(8,128)(2,1)S(1)}, bf16[2,512,768]{2,1,0:T(8,128)(2,1)}, u32[]{:S(2)}) copy-start(bf16[2,512,768]{2,1,0:T(8,128)(2,1)} %param.20) | copy-start | bytes 4718596
  542.1 58.8 %all-gather.28.cloned.1.call-start = ((), (), s32[]{:S(2)}) async-start(), calls=%async_computation.26 | async-start | bytes 3932160 | tf_op jit(solution)/shard_map/all_gather | solution.py:32
  542.8 118.8 %reduce-scatter.26.cloned.1.call-start = ((), (), s32[]{:S(2)}) async-start(), calls=%async_computation.23 | async-start | bytes 7864320 | tf_op jit(solution)/shard_map/reduce_scatter | solution.py:36
  587.2 135.5 %reduce-scatter.30.cloned.1.call-start = ((), (), s32[]{:S(2)}) async-start(), calls=%async_computation.27 | async-start | bytes 7864320 | tf_op jit(solution)/shard_map/reduce_scatter | solution.py:36
  616.2 142.4 %all-gather.26.cloned.1.call-start = ((), (), s32[]{:S(2)}) async-start(), calls=%async_computation.24 | async-start | bytes 3932160 | tf_op jit(solution)/shard_map/all_gather | solution.py:32
  661.7 60.9 %copy-start.7 = (f32[512,768]{1,0:T(8,128)S(1)}, f32[512,768]{1,0:T(8,128)}, u32[]{:S(2)}) copy-start(f32[512,768]{1,0:T(8,128)} %copy-done.6) | copy-start | bytes 4718596
  729.9 115.8 %all-gather.30.cloned.1.call-start = ((), (), s32[]{:S(2)}) async-start(), calls=%async_computation.28 | async-start | bytes 3932160 | tf_op jit(solution)/shard_map/all_gather | solution.py:32
  730.5 316.5 %reduce-scatter.42.cloned.1.call-start = ((), (), s32[]{:S(2)}) async-start(), calls=%async_computation.36 | async-start | bytes 884736
  937.5 132.2 %reduce-scatter.40.cloned.1.call-start = ((), (), s32[]{:S(2)}) async-start(), calls=%async_computation.35 | async-start | bytes 2211840
  956.5 191.1 %reduce-scatter.34.cloned.1.call-start = ((), (), s32[]{:S(2)}) async-start(), calls=%async_computation.30 | async-start | bytes 3538944 | tf_op jit(solution)/shard_map/reduce_scatter | solution.py:221
  968.2 239.5 %reduce-scatter.28.cloned.1.call-start = ((), (), s32[]{:S(2)}) async-start(), calls=%async_computation.25 | async-start | bytes 7864320 | tf_op jit(solution)/shard_map/reduce_scatter | solution.py:36
  975.7 293.1 %reduce-scatter.32.cloned.1.call-start = ((), (), s32[]{:S(2)}) async-start(), calls=%async_computation.29 | async-start | bytes 7864320 | tf_op jit(solution)/shard_map/reduce_scatter | solution.py:36
  982.8 359.1 %reduce-scatter.38.cloned.1.call-start = ((), (), s32[]{:S(2)}) async-start(), calls=%async_computation.34 | async-start | bytes 2654208 | tf_op jit(solution)/shard_map/reduce_scatter | solution.py:54
  993.4 420.7 %reduce-scatter.36.cloned.1.call-start = ((), (), s32[]{:S(2)}) async-start(), calls=%async_computation.33 | async-start | bytes 2654208 | tf_op jit(solution)/shard_map/reduce_scatter | solution.py:53
  1002.6 145.0 %copy-start.38 = (f32[3,64,512]{2,1,0:T(8,128)S(1)}, f32[3,64,512]{2,1,0:T(8,128)}, u32[]{:S(2)}) copy-start(f32[3,64,512]{2,1,0:T(8,128)} %add_divide_fusion) | copy-start | bytes 1179652
  1002.6 205.1 %copy-start.36 = (f32[512,768]{1,0:T(8,128)S(1)}, f32[512,768]{1,0:T(8,128)}, u32[]{:S(2)}) copy-start(f32[512,768]{1,0:T(8,128)} %get-tuple-element.576) | copy-start | bytes 4718596
  1071.6 197.2 %copy-start.35 = (f32[512,768]{1,0:T(8,128)S(1)}, f32[512,768]{1,0:T(8,128)}, u32[]{:S(2)}) copy-start(f32[512,768]{1,0:T(8,128)} %get-tuple-element.612) | copy-start | bytes 4718596
  (83 other events, 1102.3 us)
Sparse Core Ops, SparseCore 0:
  10.2 31.2 all-gather.33
  44.2 62.3 all-gather.13
  108.7 27.7 all-gather.31
  145.0 57.6 reduce-scatter.21
  210.9 57.3 reduce-scatter.17
  270.3 41.0 all-gather.17
  313.6 27.2 all-gather.15
  343.1 41.0 all-gather.19
  385.7 27.2 all-gather.21
  415.4 58.3 reduce-scatter.19
  476.5 58.3 reduce-scatter.23
  542.2 28.5 all-gather.23
  572.3 28.5 all-gather.27
  603.3 58.3 reduce-scatter.25
  664.2 58.3 reduce-scatter.29
  730.1 28.5 all-gather.25
  760.0 28.5 all-gather.29
  937.6 62.4 reduce-scatter.41
  1004.0 65.6 reduce-scatter.39
  1073.8 73.7 reduce-scatter.33
  1150.1 57.5 reduce-scatter.27
  1210.4 58.3 reduce-scatter.31
  1272.9 69.0 reduce-scatter.37
  1345.9 68.2 reduce-scatter.35
where the time goes:
time: 1430 us; the launch traced here: 1420 us
  waiting for transfers between devices  794 us (56%)
  matrix products  314 us (22%)
  local copies, waits for them, and re-layouts  115 us (8%)
  blocking collectives  109 us (8%)
  other arithmetic  71.4 us (5%)
  between operations  16.1 us (1%)
    reduce_scatter x8, waiting for transfers between devices, narrow(): lax.psum_scatter(partial_rows, 'head', scatter_dimension=0, tiled=True)  367 us
    all_gather x8, waiting for transfers between devices, widen(): return lax.all_gather(rows, 'head', axis=0, tiled=True)  122 us
    dot_general x12, matrix products, mat_mul(): return jnp.dot(left, right, preferred_element_type=jnp.float32)  78.1 us
    reduce_scatter x1, waiting for transfers between devices, per_device(): lax.psum_scatter(gate_total, 'dp', scatter_dimension=1, tiled=True)  74.1 us
    reduce_scatter x1, waiting for transfers between devices, settle(): lax.psum_scatter(grads[2], 'dp', scatter_dimension=0, tiled=True)  72.2 us
    reduce_scatter x1, waiting for transfers between devices, settle(): lax.psum_scatter(grads[3], 'dp', scatter_dimension=1, tiled=True)  69.5 us
    dot_general x12, matrix products, outer_rows(): lax.dot_general(left, right, (((1,), (1,)), ((), ())), preferred_element_...  48 us
    dot_general x8, matrix products, attend_back(): jnp.einsum('qhe,khe->hqk', query, key, preferred_element_type=jnp.float32)  47.5 us
  transfers between devices with their start and end apart: 24, of which 19 were waited for; matrix products, arithmetic and copies ran while one was open for 27% of the time, Pallas kernels for 0%

commit v1 on v0

v1 whole, which is shorter than its diff:
```python
import functools, math
import jax, jax.numpy as jnp
from jax import lax
from jax.experimental import pallas as pl
from jax.experimental.pallas import tpu as pltpu
from jax.sharding import PartitionSpec as P

HEAD_DIM = 64
EPS = 1e-05
F32 = jnp.float32
BF16 = jnp.bfloat16
SCALE = 1.0 / math.sqrt(HEAD_DIM)
LOG2E = math.log2(math.e)
NEG = -1e30
INV_SQRT2 = 1.0 / math.sqrt(2.0)
INV_SQRT2PI = 1.0 / math.sqrt(2.0 * math.pi)


def dot_nn(a, b):
    return lax.dot_general(a, b, (((1,), (0,)), ((), ())), preferred_element_type=F32)


def dot_nt(a, b):
    return lax.dot_general(a, b, (((1,), (1,)), ((), ())), preferred_element_type=F32)


def dot_tn(a, b):
    return lax.dot_general(a, b, (((0,), (0,)), ((), ())), preferred_element_type=F32)


def piece(ref, bits, d, flip):
    y = bits[0] ^ (d & 1)
    z1 = bits[1] ^ ((d >> 1) & 1)
    z2 = bits[2] ^ ((d >> 2) & 1)
    if flip:
        return ref.at[y, 0, z1, z2]
    return ref.at[0, y, z1, z2]


def assemble(dst, ref, bits, flip):
    rows = ref.shape[-2]
    for d in range(8):
        dst[pl.ds(d * rows, rows), :] = piece(ref, bits, d, flip)[...]


def scatter(ref, src, bits, flip):
    rows = ref.shape[-2]
    for d in range(8):
        piece(ref, bits, d, flip)[...] = src[pl.ds(d * rows, rows), :]


def spec_a(tail, pick):
    zeros = (0,) * len(tail)
    return pl.BlockSpec((1, 2, 2, 2) + tail, lambda k, *_: (pick(k), 0, 0, 0) + zeros)


def spec_b(tail, pick):
    zeros = (0,) * len(tail)
    return pl.BlockSpec((2, 1, 2, 2) + tail, lambda k, *_: (0, pick(k), 0, 0) + zeros)


def whole(shape):
    zeros = (0,) * len(shape)
    return pl.BlockSpec(shape, lambda *_: zeros)


def low_pick(k):
    return jnp.minimum(k, 1)


def high_pick(k):
    return jnp.maximum(k - 2, 0)


def norm_stats(z):
    mean = jnp.mean(z, axis=1, keepdims=True)
    centered = z - mean
    inverse = lax.rsqrt(jnp.mean(centered * centered, axis=1, keepdims=True) + EPS)
    return centered * inverse, inverse


def norm_back(du, unit, inverse):
    return inverse * (
        du
        - jnp.mean(du, axis=1, keepdims=True)
        - unit * jnp.mean(du * unit, axis=1, keepdims=True)
    )


def gelu_pair(up):
    cdf = 0.5 + 0.5 * lax.erf(up * INV_SQRT2)
    pdf = INV_SQRT2PI * jnp.exp(-0.5 * (up * up))
    return up * cdf, cdf + up * pdf


def params(mib=56, n=1):
    return pltpu.CompilerParams(
        dimension_semantics=("arbitrary",) * n, vmem_limit_bytes=mib * 1024 * 1024
    )


def ffn_fwd_kernel(chunk, bits, lens, hid, ua0, ua1, db0, db1, gain, bias, dout,
                   out, dsec, dffn, dffnt, act_o, gp_o, dgain, dbias, wu, wd, acc):
    k = pl.program_id(0)
    rows = hid.shape[0]

    @pl.when(k < 2)
    def _():
        assemble(wu, ua0, bits, False)
        assemble(wd, db0, bits, True)

    @pl.when(k >= 2)
    def _():
        assemble(wu, ua1, bits, False)
        assemble(wd, db1, bits, True)

    @pl.when(k == 0)
    def _():
        acc[...] = jnp.zeros_like(acc)

    def step(r, c):
        at = pl.ds(pl.multiple_of(r * chunk, chunk), chunk)
        up = dot_nn(hid[at, :], wu[...])
        act, gp = gelu_pair(up)
        act = act.astype(BF16)
        act_o[0, at, :] = act
        gp_o[0, at, :] = gp.astype(gp_o.dtype)
        acc[at, :] += dot_nt(act, wd[...])
        return c

    lax.fori_loop(0, rows // chunk, step, 0)

    @pl.when(k == 3)
    def _():
        dgain[...] = jnp.zeros_like(dgain)
        dbias[...] = jnp.zeros_like(dbias)
        length = rows // lens.shape[0]
        small = 128

        def fin(r, c):
            start = pl.multiple_of(r * small, small)
            at = pl.ds(start, small)
            size = lens[start // length]
            pos = (start % length) + lax.broadcasted_iota(jnp.int32, (small, 1), 0)
            valid = pos < size
            second = hid[at, :].astype(F32) + acc[at, :]
            unit, inverse = norm_stats(second)
            g = gain[...]
            out[at, :] = jnp.where(valid, unit * g + bias[...], 0.0).astype(BF16)
            dy = jnp.where(valid, dout[at, :].astype(F32), 0.0)
            dgain[...] += jnp.sum(dy * unit, axis=0, keepdims=True)
            dbias[...] += jnp.sum(dy, axis=0, keepdims=True)
            dz = norm_back(dy * g, unit, inverse)
            dsec[at, :] = dz
            low = dz.astype(BF16)
            dffn[at, :] = low
            dffnt[:, at] = low.T
            return c

        lax.fori_loop(0, rows // small, fin, 0)


def ffn_forward(bits, lens, hid, ua0, ua1, db0, db1, gain, bias, dout, chunk=512, gp_dt=F32):
    rows, width = hid.shape
    n = ua0.shape[-1]
    p = ua0.shape[-2]
    sds = jax.ShapeDtypeStruct
    return pl.pallas_call(
        functools.partial(ffn_fwd_kernel, chunk),
        out_shape=(
            sds((rows, width), BF16), sds((rows, width), F32), sds((rows, width), BF16), sds((width, rows), BF16),
            sds((4, rows, n), BF16), sds((4, rows, n), gp_dt),
            sds((1, width), F32), sds((1, width), F32),
        ),
        grid_spec=pltpu.PrefetchScalarGridSpec(
            num_scalar_prefetch=2, grid=(4,),
            in_specs=[
                whole((rows, width)),
                spec_a((p, n), low_pick), spec_a((p, n), high_pick),
                spec_b((p, n), low_pick), spec_b((p, n), high_pick),
                whole((1, width)), whole((1, width)), whole((rows, width)),
            ],
            out_specs=[
                whole((rows, width)), whole((rows, width)), whole((rows, width)), whole((width, rows)),
                pl.BlockSpec((1, rows, n), lambda k, *_: (k, 0, 0)),
                pl.BlockSpec((1, rows, n), lambda k, *_: (k, 0, 0)),
                whole((1, width)), whole((1, width)),
            ],
            scratch_shapes=[
                pltpu.VMEM((width, n), BF16), pltpu.VMEM((width, n), BF16),
                pltpu.VMEM((rows, width), F32),
            ],
        ),
        compiler_params=params(),
        cost_estimate=pl.CostEstimate(
            flops=4 * rows * width * 4 * n, bytes_accessed=40 * rows * width, transcendentals=0
        ),
    )(bits, lens, hid, ua0, ua1, db0, db1, gain, bias, dout)


def ffn_bwd_kernel(chunk, last, bits, ht, dt, dffn, ua, db, act, gp, *rest):
    if last:
        dsec, part, unit, inverse, gain, gu, gd, dfirst, dattn, dattnt, dgain, dbias, wu, wd, dup_s, acc, tmp = rest
    else:
        gu, gd, dh_o, wu, wd, dup_s, acc, tmp = rest
    k = pl.program_id(0)
    rows, width = dffn.shape

    assemble(wu, ua, bits, False)
    assemble(wd, db, bits, True)

    @pl.when(k == 0)
    def _():
        if last:
            acc[...] = part[...] + dsec[...]
        else:
            acc[...] = jnp.zeros_like(acc)

    def step(r, c):
        at = pl.ds(pl.multiple_of(r * chunk, chunk), chunk)
        dact = dot_nn(dffn[at, :], wd[...])
        dup = (dact * gp[0, at, :].astype(F32)).astype(BF16)
        dup_s[at, :] = dup
        acc[at, :] += dot_nt(dup, wu[...])
        return c

    lax.fori_loop(0, rows // chunk, step, 0)

    tmp[...] = dot_nn(ht[...], dup_s[...]).astype(BF16)
    scatter(gu, tmp, bits, False)
    tmp[...] = dot_nn(dt[...], act[0]).astype(BF16)
    scatter(gd, tmp, bits, True)

    @pl.when(k == 1)
    def _():
        if not last:
            dh_o[...] = acc[...]
        else:
            dgain[...] = jnp.zeros_like(dgain)
            dbias[...] = jnp.zeros_like(dbias)
            small = 128

            def fin(r, c):
                at = pl.ds(pl.multiple_of(r * small, small), small)
                dh = acc[at, :]
                u = unit[at, :]
                dgain[...] += jnp.sum(dh * u, axis=0, keepdims=True)
                dbias[...] += jnp.sum(dh, axis=0, keepdims=True)
                dz = norm_back(dh * gain[...], u, inverse[at, :])
                dfirst[at, :] = dz
                low = dz.astype(BF16)
                dattn[at, :] = low
                dattnt[:, at] = low.T
                return c

            lax.fori_loop(0, rows // small, fin, 0)


def ffn_backward(last, bits, ht, dt, dffn, ua, db, act, gp, extra=(), chunk=512):
    rows, width = dffn.shape
    n = ua.shape[-1]
    p = ua.shape[-2]
    sds = jax.ShapeDtypeStruct
    half = (1 - last) * 2
    pick = lambda k: k
    out_shape = [sds((2, 2, 2, 2, p, n), BF16), sds((2, 2, 2, 2, p, n), BF16)]
    out_specs = [spec_a((p, n), pick), spec_b((p, n), pick)]
    in_specs = [
        whole((width, rows)), whole((width, rows)), whole((rows, width)),
        spec_a((p, n), pick), spec_b((p, n), pick),
        pl.BlockSpec((1, rows, n), lambda k, *_: (k + half, 0, 0)),
        pl.BlockSpec((1, rows, n), lambda k, *_: (k + half, 0, 0)),
    ]
    if last:
        in_specs += [whole((rows, width))] * 3 + [whole((rows, 1)), whole((1, width))]
        out_shape += [sds((rows, width), F32), sds((rows, width), BF16), sds((width, rows), BF16), sds((1, width), F32), sds((1, width), F32)]
        out_specs += [whole((rows, width))] * 2 + [whole((width, rows))] + [whole((1, width))] * 2
    else:
        out_shape += [sds((rows, width), F32)]
        out_specs += [whole((rows, width))]
    return pl.pallas_call(
        functools.partial(ffn_bwd_kernel, chunk, last),
        out_shape=out_shape,
        grid_spec=pltpu.PrefetchScalarGridSpec(
            num_scalar_prefetch=1, grid=(2,), in_specs=in_specs, out_specs=out_specs,
            scratch_shapes=[
                pltpu.VMEM((width, n), BF16), pltpu.VMEM((width, n), BF16),
                pltpu.VMEM((rows, n), BF16), pltpu.VMEM((rows, width), F32),
                pltpu.VMEM((width, n), BF16),
            ],
        ),
        compiler_params=params(),
        cost_estimate=pl.CostEstimate(
            flops=8 * rows * width * 2 * n, bytes_accessed=30 * rows * width, transcendentals=0
        ),
    )(bits, ht, dt, dffn, ua, db, act, gp, *extra)


def key_bias(size, length):
    pos = lax.broadcasted_iota(jnp.int32, (1, length), 1)
    return jnp.where(pos < size, 0.0, NEG).astype(F32)


def gate_rows(ga, gb, bits, i, d0, count):
    parts = []
    for j in range(count):
        d = d0 + j
        y = bits[0] ^ (d & 1)
        z1 = bits[1] ^ ((d >> 1) & 1)
        z2 = bits[2] ^ ((d >> 2) & 1)
        parts.append(ga[0, y, z1, z2, i])
        parts.append(gb[y, 0, z1, z2, i])
    return jnp.concatenate(parts, axis=0).astype(F32)


def att_fwd_kernel(chunk, bits, lens, qk, v, ga, gb, mixed, lse):
    length = qk.shape[1]
    heads = v.shape[2] // HEAD_DIM
    size = lens[pl.program_id(1)]
    bias = key_bias(size, length)
    per = 2 * ga.shape[-2]

    def step(r, c):
        at = pl.ds(pl.multiple_of(r * chunk, chunk), chunk)
        outs = []
        stats = []
        for i in range(heads):
            q = qk[0, at, pl.ds(i * HEAD_DIM, HEAD_DIM)]
            key = qk[0, :, pl.ds((heads + i) * HEAD_DIM, HEAD_DIM)]
            s = dot_nt(q, key) * (SCALE * LOG2E) + bias
            top = jnp.max(s, axis=1, keepdims=True)
            e = jnp.exp2(s - top)
            total = jnp.sum(e, axis=1, keepdims=True)
            g = gate_rows(ga, gb, bits, i, r * (chunk // per), chunk // per)
            w = (e * (1.0 / total) * g).astype(BF16)
            outs.append(dot_nn(w, v[0, :, pl.ds(i * HEAD_DIM, HEAD_DIM)]))
            stats.append(top + jnp.log2(total))
        mixed[0, at, :] = jnp.concatenate(outs, axis=1).astype(BF16)
        lse[0, at, :] = jnp.concatenate(stats, axis=1)
        return c

    for r in range(length // chunk):
        step(r, 0)


def attention_forward(half, bits, lens, qk, v, ga, gb, chunk=512):
    _, rows, w2 = qk.shape
    w1 = v.shape[2]
    count = lens.shape[0]
    length = rows // count
    heads, sub, keys = ga.shape[-3:]
    sds = jax.ShapeDtypeStruct
    off = half * 2
    return pl.pallas_call(
        functools.partial(att_fwd_kernel, chunk),
        out_shape=(sds((2, rows, w1), BF16), sds((2, rows, heads), F32)),
        grid_spec=pltpu.PrefetchScalarGridSpec(
            num_scalar_prefetch=2, grid=(2, count),
            in_specs=[
                pl.BlockSpec((1, length, w2), lambda k, s, *_: (k + off, s, 0)),
                pl.BlockSpec((1, length, w1), lambda k, s, *_: (k + off, s, 0)),
                spec_a((heads, sub, keys), lambda k: k), spec_b((heads, sub, keys), lambda k: k),
            ],
            out_specs=[
                pl.BlockSpec((1, length, w1), lambda k, s, *_: (k, s, 0)),
                pl.BlockSpec((1, length, heads), lambda k, s, *_: (k, s, 0)),
            ],
        ),
        compiler_params=params(n=2),
        cost_estimate=pl.CostEstimate(
            flops=16 * 2 * rows * length * w1, bytes_accessed=16 * rows * w1, transcendentals=0
        ),
    )(bits, lens, qk, v, ga, gb)


def att_bwd_kernel(chunk, bits, lens, qk, v, ga, gb, lse, dattn, wo,
                   dqk, dv, oga, ogb, dm_s, dmt, qt, acc, dvt, dkt):
    length = qk.shape[1]
    heads = v.shape[2] // HEAD_DIM
    hw = heads * HEAD_DIM
    seq = pl.program_id(1)
    size = lens[seq]
    bias = key_bias(size, length)
    per = 2 * ga.shape[-2]

    dm = dot_nn(dattn[...], wo[0]).astype(BF16)
    dm_s[...] = dm
    dmt[...] = dm.T
    qt[...] = qk[0, :, pl.ds(0, hw)].T
    dvt[...] = jnp.zeros_like(dvt)
    dkt[...] = jnp.zeros_like(dkt)

    @pl.when(seq == 0)
    def _():
        acc[...] = jnp.zeros_like(acc)

    for r in range(length // chunk):
        at = pl.ds(r * chunk, chunk)
        dqs = []
        for i in range(heads):
            cols = pl.ds(i * HEAD_DIM, HEAD_DIM)
            q = qk[0, at, cols]
            key = qk[0, :, pl.ds((heads + i) * HEAD_DIM, HEAD_DIM)]
            p = jnp.exp2(dot_nt(q, key) * (SCALE * LOG2E) + bias - lse[0, at, pl.ds(i, 1)])
            g = gate_rows(ga, gb, bits, i, r * (chunk // per), chunk // per)
            w = (p * g).astype(BF16)
            dw = dot_nt(dm_s[at, cols], v[0, :, cols])
            t = dw * p
            acc[i, at, :] += t
            u = t * g
            ds = (u - p * jnp.sum(u, axis=1, keepdims=True)).astype(BF16)
            dqs.append(dot_nn(ds, key) * SCALE)
            dvt[cols, :] += dot_nn(dmt[cols, at], w)
            dkt[cols, :] += dot_nn(qt[cols, at], ds)
        dqk[0, at, pl.ds(0, hw)] = jnp.concatenate(dqs, axis=1).astype(BF16)

    dqk[0, :, pl.ds(hw, hw)] = (dkt[...] * SCALE).astype(BF16).T
    dv[0] = dvt[...].astype(BF16).T

    @pl.when(seq == pl.num_programs(1) - 1)
    def _():
        sub = per // 2
        for d in range(length // per):
            y = bits[0] ^ (d & 1)
            z1 = bits[1] ^ ((d >> 1) & 1)
            z2 = bits[2] ^ ((d >> 2) & 1)
            for i in range(heads):
                oga[0, y, z1, z2, i] = acc[i, pl.ds(d * per, sub), :].astype(oga.dtype)
                ogb[y, 0, z1, z2, i] = acc[i, pl.ds(d * per + sub, sub), :].astype(ogb.dtype)


def attention_backward(half, bits, lens, qk, v, ga, gb, lse, dattn, wo, chunk=512):
    _, rows, w2 = qk.shape
    w1 = v.shape[2]
    width = dattn.shape[1]
    count = lens.shape[0]
    length = rows // count
    heads, sub, keys = ga.shape[-3:]
    sds = jax.ShapeDtypeStruct
    off = half * 2
    gates = (2, 2, 2, 2, heads, sub, keys)
    return pl.pallas_call(
        functools.partial(att_bwd_kernel, chunk),
        out_shape=(sds((2, rows, w2), BF16), sds((2, rows, w1), BF16), sds(gates, BF16), sds(gates, BF16)),
        grid_spec=pltpu.PrefetchScalarGridSpec(
            num_scalar_prefetch=2, grid=(2, count),
            in_specs=[
                pl.BlockSpec((1, length, w2), lambda k, s, *_: (k + off, s, 0)),
                pl.BlockSpec((1, length, w1), lambda k, s, *_: (k + off, s, 0)),
                spec_a((heads, sub, keys), lambda k: k), spec_b((heads, sub, keys), lambda k: k),
                pl.BlockSpec((1, length, heads), lambda k, s, *_: (k, s, 0)),
                pl.BlockSpec((length, width), lambda k, s, *_: (s, 0)),
                pl.BlockSpec((1, width, w1), lambda k, s, *_: (k + off, 0, 0)),
            ],
            out_specs=[
                pl.BlockSpec((1, length, w2), lambda k, s, *_: (k, s, 0)),
                pl.BlockSpec((1, length, w1), lambda k, s, *_: (k, s, 0)),
                spec_a((heads, sub, keys), lambda k: k), spec_b((heads, sub, keys), lambda k: k),
            ],
            scratch_shapes=[
                pltpu.VMEM((length, w1), BF16), pltpu.VMEM((w1, length), BF16),
                pltpu.VMEM((w1, length), BF16), pltpu.VMEM((heads, length, keys), F32),
                pltpu.VMEM((w1, keys), F32), pltpu.VMEM((w1, keys), F32),
            ],
        ),
        compiler_params=params(n=2),
        cost_estimate=pl.CostEstimate(
            flops=40 * 2 * rows * length * w1, bytes_accessed=30 * rows * w1, transcendentals=0
        ),
    )(bits, lens, qk, v, ga, gb, lse, dattn, wo)


def qkv_kernel(bits, x, wa0, wa1, wb0, wb1, qk, v, wqk, wv, wo, xt, wb):
    k = pl.program_id(0)
    w2 = qk.shape[2]
    w1 = v.shape[2]

    @pl.when(k < 2)
    def _():
        assemble(wqk.at[0], wa0, bits, False)
        assemble(wb, wb0, bits, True)

    @pl.when(k >= 2)
    def _():
        assemble(wqk.at[0], wa1, bits, False)
        assemble(wb, wb1, bits, True)

    @pl.when(k == 0)
    def _():
        xt[...] = x[...].T

    wv[0] = wb[:, pl.ds(0, w1)]
    wo[0] = wb[:, pl.ds(w1, w1)]
    qk[0] = dot_nn(x[...], wqk[0]).astype(BF16)
    v[0] = dot_nn(x[...], wv[0]).astype(BF16)


def project(bits, x, wa0, wa1, wb0, wb1):
    rows, width = x.shape
    p, w2 = wa0.shape[-2:]
    w1 = w2 // 2
    sds = jax.ShapeDtypeStruct
    head = lambda s: pl.BlockSpec((1,) + s, lambda k, *_: (k, 0, 0))
    return pl.pallas_call(
        qkv_kernel,
        out_shape=(sds((4, rows, w2), BF16), sds((4, rows, w1), BF16), sds((4, width, w2), BF16),
                   sds((4, width, w1), BF16), sds((4, width, w1), BF16), sds((width, rows), BF16)),
        grid_spec=pltpu.PrefetchScalarGridSpec(
            num_scalar_prefetch=1, grid=(4,),
            in_specs=[whole((rows, width)), spec_a((p, w2), low_pick), spec_a((p, w2), high_pick),
                      spec_b((p, w2), low_pick), spec_b((p, w2), high_pick)],
            out_specs=[head((rows, w2)), head((rows, w1)), head((width, w2)), head((width, w1)), head((width, w1)),
                       whole((width, rows))],
            scratch_shapes=[pltpu.VMEM((width, w2), BF16)],
        ),
        compiler_params=params(),
        cost_estimate=pl.CostEstimate(flops=2 * rows * width * 4 * (w1 + w2), bytes_accessed=16 * rows * width, transcendentals=0),
    )(bits, x, wa0, wa1, wb0, wb1)


def out_kernel(x, m0, m1, wo, gain, bias, hid, unit, inverse, hidt):
    attn = dot_nt(m0[0], wo[0]) + dot_nt(m0[1], wo[1]) + dot_nt(m1[0], wo[2]) + dot_nt(m1[1], wo[3])
    u, inv = norm_stats(x[...].astype(F32) + attn)
    h = (u * gain[...] + bias[...]).astype(BF16)
    hid[...] = h
    hidt[...] = h.T
    unit[...] = u
    inverse[...] = inv


def out_forward(x, m0, m1, wo, gain, bias, block=256):
    rows, width = x.shape
    w1 = wo.shape[2]
    sds = jax.ShapeDtypeStruct
    row = lambda w: pl.BlockSpec((block, w), lambda r: (r, 0))
    mix = pl.BlockSpec((2, block, w1), lambda r: (0, r, 0))
    return pl.pallas_call(
        out_kernel,
        grid=(rows // block,),
        out_shape=(sds((rows, width), BF16), sds((rows, width), F32), sds((rows, 1), F32), sds((width, rows), BF16)),
        in_specs=[row(width), mix, mix, whole((4, width, w1)), whole((1, width)), whole((1, width))],
        out_specs=[row(width), row(width), row(1), pl.BlockSpec((width, block), lambda r: (0, r))],
        compiler_params=params(),
        cost_estimate=pl.CostEstimate(flops=2 * rows * width * 4 * w1, bytes_accessed=12 * rows * width, transcendentals=0),
    )(x, m0, m1, wo, gain, bias)


def qkv_grad_kernel(bits, xt, dat, dqk, dv, mixed, ga, gb, tmp):
    w1 = dv.shape[2]
    tmp[...] = dot_nn(xt[...], dqk[0]).astype(BF16)
    scatter(ga, tmp, bits, False)
    tmp[:, pl.ds(0, w1)] = dot_nn(xt[...], dv[0]).astype(BF16)
    tmp[:, pl.ds(w1, w1)] = dot_nn(dat[...], mixed[0]).astype(BF16)
    scatter(gb, tmp, bits, True)


def qkv_grads(bits, xt, dat, dqk, dv, mixed):
    width, rows = xt.shape
    w2 = dqk.shape[2]
    w1 = dv.shape[2]
    per = width // 8
    sds = jax.ShapeDtypeStruct
    pick = lambda k: k
    head = lambda w: pl.BlockSpec((1, rows, w), lambda k, *_: (k, 0, 0))
    return pl.pallas_call(
        qkv_grad_kernel,
        out_shape=(sds((2, 2, 2, 2, per, w2), BF16), sds((2, 2, 2, 2, per, w2), BF16)),
        grid_spec=pltpu.PrefetchScalarGridSpec(
            num_scalar_prefetch=1, grid=(2,),
            in_specs=[whole((width, rows)), whole((width, rows)), head(w2), head(w1), head(w1)],
            out_specs=[spec_a((per, w2), pick), spec_b((per, w2), pick)],
            scratch_shapes=[pltpu.VMEM((width, w2), BF16)],
        ),
        compiler_params=params(),
        cost_estimate=pl.CostEstimate(flops=2 * rows * width * 2 * 2 * w2, bytes_accessed=8 * rows * width, transcendentals=0),
    )(bits, xt, dat, dqk, dv, mixed)


def dinput_kernel(dfirst, dqk0, dqk1, dv0, dv1, wqk, wv, out):
    total = dfirst[...]
    for k, (a, b) in enumerate(((dqk0, dv0), (dqk0, dv0), (dqk1, dv1), (dqk1, dv1))):
        total = total + dot_nt(a[k % 2], wqk[k]) + dot_nt(b[k % 2], wv[k])
    out[...] = total


def input_backward(dfirst, dqk0, dqk1, dv0, dv1, wqk, wv, block=256):
    rows, width = dfirst.shape
    w2 = wqk.shape[2]
    w1 = wv.shape[2]
    row = pl.BlockSpec((block, width), lambda r: (r, 0))
    part = lambda w: pl.BlockSpec((2, block, w), lambda r: (0, r, 0))
    return pl.pallas_call(
        dinput_kernel,
        grid=(rows // block,),
        out_shape=jax.ShapeDtypeStruct((rows, width), F32),
        in_specs=[row, part(w2), part(w2), part(w1), part(w1), whole((4, width, w2)), whole((4, width, w1))],
        out_specs=row,
        compiler_params=params(),
        cost_estimate=pl.CostEstimate(flops=2 * rows * width * 4 * (w1 + w2), bytes_accessed=14 * rows * width, transcendentals=0),
    )(dfirst, dqk0, dqk1, dv0, dv1, wqk, wv)


GROUPS = 8


def partner_dp(value, bit):
    size = lax.axis_size("dp")
    step = (1 << bit) * (size // GROUPS)
    return lax.ppermute(value, "dp", [(i, i ^ step) for i in range(size)])


def partner_head(value, bit):
    size = lax.axis_size("head")
    return lax.ppermute(value, "head", [(i, i ^ (1 << bit)) for i in range(size)])


def over_y(value):
    return partner_dp(value, 0)


def over_near(value):
    return partner_dp(value, 1)


def over_far(value):
    return partner_dp(value, 2)


def over_pair(value):
    return partner_head(value, 0)


def over_x(value):
    return partner_head(value, 1)


def inner_groups():
    inner = lax.axis_size("dp") // GROUPS
    return inner, [[g * inner + i for i in range(inner)] for g in range(GROUPS)]


def inner_gather(value, axis):
    inner, groups = inner_groups()
    if inner == 1:
        return value
    return lax.all_gather(value, "dp", axis_index_groups=groups, axis=axis, tiled=True)


def inner_scatter(value, axis):
    inner, groups = inner_groups()
    if inner == 1:
        return value
    return lax.psum_scatter(value, "dp", axis_index_groups=groups, scatter_dimension=axis, tiled=True)


def spread(a, b):
    both = jnp.stack([a, b])
    both = jnp.stack([both, over_far(both)], axis=1)
    both = jnp.stack([both, over_near(both)], axis=1)
    a, b = both[0], both[1]
    a = jnp.stack([a, over_y(a)])
    b = jnp.stack([b, over_x(b)])
    a = jnp.stack([a, over_x(a)])
    b = jnp.stack([b, over_y(b)])
    return a, over_pair(a), b, over_pair(b)


def wide(value):
    return value.astype(F32)


def collect(a_keep, a_send, b_keep, b_send):
    ra, rb = over_pair(a_send), over_pair(b_send)
    sa = over_x((wide(a_keep[1]) + wide(ra[1])).astype(BF16))
    sb = over_y((wide(b_keep[1]) + wide(rb[1])).astype(BF16))
    ta = over_y((wide(a_keep[0, 1]) + wide(ra[0, 1]) + wide(sa[1])).astype(BF16))
    tb = over_x((wide(b_keep[0, 1]) + wide(rb[0, 1]) + wide(sb[1])).astype(BF16))
    a = wide(a_keep[0, 0]) + wide(ra[0, 0]) + wide(sa[0]) + wide(ta)
    b = wide(b_keep[0, 0]) + wide(rb[0, 0]) + wide(sb[0]) + wide(tb)
    u = over_near(jnp.stack([a[1], b[1]]).astype(BF16))
    w = over_far(jnp.stack([a[0, 1] + wide(u[0, 1]), b[0, 1] + wide(u[1, 1])]).astype(BF16))
    return a[0, 0] + wide(u[0, 0]) + wide(w[0]), b[0, 0] + wide(u[1, 0]) + wide(w[1])


def total_everywhere(value):
    for name in ("head", "dp"):
        size = lax.axis_size(name)
        step = 1
        while step < size:
            value = value + lax.ppermute(value, name, [(i, i ^ step) for i in range(size)])
            step *= 2
    return value


def per_device(layer_input, output_grad, lengths, w_qkv, w_out, w_up, w_down,
               norm_gains, norm_biases, mask_logits, mask_noise):
    micro, seq, width = layer_input.shape
    rows = micro * seq
    x = layer_input.reshape(rows, width)
    dout = output_grad.reshape(rows, width)
    place = lax.axis_index("dp") // (lax.axis_size("dp") // GROUPS)
    bits = jnp.stack([place & 1, (place >> 1) & 1, (place >> 2) & 1]).astype(jnp.int32)
    lens = lax.dynamic_slice_in_dim(lengths, lax.axis_index("head"), 1, 1).reshape(micro)

    gate_part = jax.nn.sigmoid(mask_logits + mask_noise)
    gate_all = inner_gather(gate_part.astype(BF16), 1)
    sub = gate_all.shape[1] // 2
    first = spread(
        inner_gather(jnp.concatenate([w_qkv[0], w_qkv[1]], axis=1), 0),
        inner_gather(jnp.concatenate([w_qkv[2], w_out.T], axis=1), 0),
    )
    gates = spread(gate_all[:, :sub], gate_all[:, sub:])
    ffn = spread(inner_gather(w_up, 0), inner_gather(w_down.T, 0))

    gain1, gain2 = norm_gains[0:1], norm_gains[1:2]
    bias1, bias2 = norm_biases[0:1], norm_biases[1:2]
    qk, v, wqk, wv, wo, xt = project(bits, x, *first)
    m0, lse0 = attention_forward(0, bits, lens, qk, v, gates[0], gates[2])
    m1, lse1 = attention_forward(1, bits, lens, qk, v, gates[1], gates[3])
    hid, unit, inverse, hidt = out_forward(x, m0, m1, wo, gain1, bias1)
    out, dsec, dffn, dffnt, act, gp, dgain2, dbias2 = ffn_forward(
        bits, lens, hid, *ffn, gain2, bias2, dout
    )
    up1, down1, partial = ffn_backward(False, bits, hidt, dffnt, dffn, ffn[1], ffn[3], act, gp)
    up0, down0, dfirst, dattn, dattnt, dgain1, dbias1 = ffn_backward(
        True, bits, hidt, dffnt, dffn, ffn[0], ffn[2], act, gp, (dsec, partial, unit, inverse, gain1)
    )
    up_grad, down_grad = collect(up0, up1, down0, down1)
    norms = total_everywhere(jnp.concatenate([dgain1, dgain2, dbias1, dbias2]))
    dqk1, dv1, ga1, gb1 = attention_backward(1, bits, lens, qk, v, gates[1], gates[3], lse1, dattn, wo)
    qka1, vo1 = qkv_grads(bits, xt, dattnt, dqk1, dv1, m1)
    dqk0, dv0, ga0, gb0 = attention_backward(0, bits, lens, qk, v, gates[0], gates[2], lse0, dattn, wo)
    gate_a, gate_b = collect(ga0, ga1, gb0, gb1)
    qka0, vo0 = qkv_grads(bits, xt, dattnt, dqk0, dv0, m0)
    qk_grad, vo_grad = collect(qka0, qka1, vo0, vo1)
    dinput = input_backward(dfirst, dqk0, dqk1, dv0, dv1, wqk, wv)

    qk_grad, vo_grad = inner_scatter(qk_grad, 0), inner_scatter(vo_grad, 0)
    local = vo_grad.shape[1] // 2
    gate_grad = inner_scatter(jnp.concatenate([gate_a, gate_b], axis=1), 1)
    return (
        out.reshape(micro, seq, width),
        dinput.reshape(micro, seq, width),
        jnp.stack([qk_grad[:, :local], qk_grad[:, local:], vo_grad[:, :local]]),
        vo_grad[:, local:].T,
        inner_scatter(up_grad, 0),
        inner_scatter(down_grad, 0).T,
        norms[:2],
        norms[2:],
        gate_grad * gate_part * (1.0 - gate_part),
    )


def solution(mesh):
    rows = P(None, ("dp", "head"), None)
    gates = P("head", "dp", None)
    weights = (P(None, "dp", "head"), P("head", "dp"), P("dp", "head"), P("head", "dp"))
    return jax.shard_map(
        per_device,
        mesh=mesh,
        in_specs=(rows, rows, P(None, "dp")) + weights + (P(), P(), gates, gates),
        out_specs=(rows, rows) + weights + (P(), P(), gates),
        check_vma=False,
    )
```

time: 1430 us -> 472 us (0.33)
  waiting for transfers between devices: 794 us -> 191 us
  matrix products: 314 us -> 0 us
  Pallas kernels: 0 us -> 184 us
  blocking collectives: 109 us -> 0 us
  local copies, waits for them, and re-layouts: 115 us -> 8.27 us
  starting transfers between devices: 2.09 us -> 52.6 us
  other arithmetic: 71.4 us -> 29.9 us
  between operations: 16.1 us -> 1.56 us
    reduce_scatter x11 -> x0, waiting for transfers between devices: 583 us -> none  [the longest x8 367 us: narrow(): lax.psum_scatter(partial_rows, 'head', scatter_dimension=0, tiled=True)]
    dot_general x92 -> x0, matrix products: 314 us -> none  [the longest x12 78.1 us: mat_mul(): return jnp.dot(left, right, preferred_element_type=jnp.float32)]
    ppermute x0 -> x53, waiting for transfers between devices: none -> 191 us  [the longest x24 144 us: partner_dp(): return lax.ppermute(value, 'dp', [(i, i ^ step) for i in range(size)])]
    all_gather x11 -> x0, waiting for transfers between devices: 186 us -> none  [the longest x8 122 us: widen(): return lax.all_gather(rows, 'head', axis=0, tiled=True)]
    pallas_call x0 -> x12, Pallas kernels: none -> 184 us  [the longest x2 46.1 us: ffn_backward(): pl.pallas_call(functools.partial(ffn_bwd_kernel, chunk, last), out_shape=...]
    all_gather x2 -> x0, blocking collectives: 68.9 us -> none  [the longest x1 37.1 us: fetch(): lax.all_gather(w_qkv, 'dp', axis=1, tiled=True)]
    ppermute x0 -> x53, starting transfers between devices: none -> 52.6 us  [the longest x24 32.5 us: partner_dp(): return lax.ppermute(value, 'dp', [(i, i ^ step) for i in range(size)])]
    psum x1 -> x0, blocking collectives: 40.1 us -> none  [per_device(): gain_sum, bias_sum = lax.psum((gain_total, bias_total), ('dp', 'head'))]
  transfers between devices with their start and end apart: 24 -> 53, of which waited for: 19 -> 25; matrix products, arithmetic and copies ran while one was open for 27% -> 7% of each run, Pallas kernels for 0% -> 24%
where the time goes in v1:
time: 472 us; the launch traced here: 467 us
  waiting for transfers between devices  191 us (40%)
  Pallas kernels  184 us (39%)
  starting transfers between devices  52.6 us (11%)
  other arithmetic  29.9 us (6%)
  local copies, waits for them, and re-layouts  8.27 us (2%)
    ppermute x24, waiting for transfers between devices, partner_dp(): return lax.ppermute(value, 'dp', [(i, i ^ step) for i in range(size)])  144 us
    ppermute x24, waiting for transfers between devices, partner_head(): return lax.ppermute(value, 'head', [(i, i ^ 1 << bit) for i in range(size)])  47.2 us
    pallas_call x2, Pallas kernels, ffn_backward(): pl.pallas_call(functools.partial(ffn_bwd_kernel, chunk, last), out_shape=...  46.1 us
    pallas_call x2, Pallas kernels, attention_backward(): pl.pallas_call(functools.partial(att_bwd_kernel, chunk), out_shape=(sds((...  39.4 us
    ppermute x24, starting transfers between devices, partner_dp(): return lax.ppermute(value, 'dp', [(i, i ^ step) for i in range(size)])  32.5 us
    pallas_call x1, Pallas kernels, ffn_forward(): pl.pallas_call(functools.partial(ffn_fwd_kernel, chunk), out_shape=(sds((...  27.5 us
    pallas_call x2, Pallas kernels, attention_forward(): pl.pallas_call(functools.partial(att_fwd_kernel, chunk), out_shape=(sds((...  23.7 us
    pallas_call x2, Pallas kernels, qkv_grads(): pl.pallas_call(qkv_grad_kernel, out_shape=(sds((2, 2, 2, 2, per, w2), BF1...  16.8 us
  transfers between devices with their start and end apart: 53, of which 25 were waited for; matrix products, arithmetic and copies ran while one was open for 7% of the time, Pallas kernels for 24%

profile of v1, /device:TPU:0, one launch (start us, length us, event | category | flops | bytes accessed | tf_op | source)
XLA Modules:
  0.0 467.4 jit_solution(12172131426575772443)
XLA Ops:
  1.7 4.1 collective-permute-start.16
  7.7 11.4 %collective-permute-done.16 = bf16[2,96,768]{2,1,0:T(8,128)(2,1)S(1)} collective-permute-done((bf16[2,96,768]{2,1,0:T(8,128)(2,1)S(1)}, bf16[2,96,768]{2,1,0:T(8,128)(2,1)S(1)}, u32[]{:S(2)}, u32[]{:S(2)}) %collective-permute-start.16) | collective-permute-done | bytes 294944 | tf_op jit(solution)/shard_map/ppermute | solution.py:609
  23.6 13.3 %collective-permute-done.17 = bf16[2,2,96,768]{3,2,1,0:T(8,128)(2,1)S(1)} collective-permute-done((bf16[2,2,96,768]{3,2,1,0:T(8,128)(2,1)S(1)}, bf16[2,2,96,768]{3,2,1,0:T(8,128)(2,1)S(1)}, u32[]{:S(2)}, u32[]{:S(2)}) %collective-permute-start.17) | collective-permute-done | bytes 589856 | tf_op jit(solution)/shard_map/ppermute | solution.py:609
  43.7 5.7 %collective-permute-done.8 = bf16[2,3,32,512]{3,2,1,0:T(8,128)(2,1)S(1)} collective-permute-done((bf16[2,3,32,512]{3,2,1,0:T(8,128)(2,1)S(1)}, bf16[2,3,32,512]{3,2,1,0:T(8,128)(2,1)S(1)}, u32[]{:S(2)}, u32[]{:S(2)}) %collective-permute-start.8) | collective-permute-done | bytes 196640 | tf_op jit(solution)/shard_map/ppermute | solution.py:609
  55.0 5.1 %collective-permute-done.9 = bf16[2,2,3,32,512]{4,3,2,1,0:T(8,128)(2,1)S(1)} collective-permute-done((bf16[2,2,3,32,512]{4,3,2,1,0:T(8,128)(2,1)S(1)}, bf16[2,2,3,32,512]{4,3,2,1,0:T(8,128)(2,1)S(1)}, u32[]{:S(2)}, u32[]{:S(2)}) %collective-permute-start.9) | collective-permute-done | bytes 393248 | tf_op jit(solution)/shard_map/ppermute | solution.py:609
  73.9 30.4 %collective-permute-done.6 = bf16[2,2,2,96,384]{4,3,2,1,0:T(8,128)(2,1)S(1)} collective-permute-done((bf16[2,2,2,96,384]{4,3,2,1,0:T(8,128)(2,1)S(1)}, bf16[2,2,2,96,384]{4,3,2,1,0:T(8,128)(2,1)S(1)}, u32[]{:S(2)}, u32[]{:S(2)}) %collective-permute-start.6) | collective-permute-done | bytes 589856 | tf_op jit(solution)/shard_map/ppermute | solution.py:609
  106.0 4.7 collective-permute-done.2
  110.7 8.3 %collective-permute-done.10 = bf16[2,2,3,32,512]{4,3,2,1,0:T(8,128)(2,1)S(1)} collective-permute-done((bf16[2,2,3,32,512]{4,3,2,1,0:T(8,128)(2,1)S(1)}, bf16[2,2,3,32,512]{4,3,2,1,0:T(8,128)(2,1)S(1)}, u32[]{:S(2)}, u32[]{:S(2)}) %collective-permute-start.10) | collective-permute-done | bytes 393248 | tf_op jit(solution)/shard_map/ppermute | solution.py:609
  123.6 11.7 %collective-permute-done.3 = bf16[2,2,2,96,384]{4,3,2,1,0:T(8,128)(2,1)S(1)} collective-permute-done((bf16[2,2,2,96,384]{4,3,2,1,0:T(8,128)(2,1)S(1)}, bf16[2,2,2,96,384]{4,3,2,1,0:T(8,128)(2,1)S(1)}, u32[]{:S(2)}, u32[]{:S(2)}) %collective-permute-start.3) | collective-permute-done | bytes 589856 | tf_op jit(solution)/shard_map/ppermute | solution.py:614
  138.3 9.7 %collective-permute-done.11 = bf16[2,2,2,3,32,512]{5,4,3,2,1,0:T(8,128)(2,1)S(1)} collective-permute-done((bf16[2,2,2,3,32,512]{5,4,3,2,1,0:T(8,128)(2,1)S(1)}, bf16[2,2,2,3,32,512]{5,4,3,2,1,0:T(8,128)(2,1)S(1)}, u32[]{:S(2)}, u32[]{:S(2)}) %collective-permute-start.11) | collective-permute-done | bytes 786464 | tf_op jit(solution)/shard_map/ppermute | solution.py:614
  152.7 12.5 %shard_map.178 = (bf16[4,1024,384]{2,1,0:T(8,128)(2,1)}, bf16[4,1024,192]{2,1,0:T(8,128)(2,1)}, bf16[4,768,384]{2,1,0:T(8,128)(2,1)}, bf16[4,768,192]{2,1,0:T(8,...) custom-call(s32[3]{0:T(128)} %pad_add_fusion.bits, bf16[1024,768]{1,0:T(8,128)(2,1)} %bitcast.265, ...), custom_call_target="tpu_custom_call" | custom-call | flops 3623878656 | bytes 12582912 | tf_op jit(solution)/shard_map/pallas_call | solution.py:504
  165.1 11.8 %shard_map.179 = (bf16[2,1024,192]{2,1,0:T(8,128)(2,1)}, f32[2,1024,3]{2,1,0:T(8,128)}) custom-call(s32[3]{0:T(128)} %pad_add_fusion.bits, s32[2]{0:T(128)} %dynamic-slice_reduce_fusion.lens, bf16[4,1024,384]{2,1,0:T(8,128)(2,1)} %get-tuple-element.53.qk, bf16[4,1024,192]{2,1,0:T(8,128)(2,1)} %get-tuple-element.54.v, ...), custom_call_target="tpu_custom_call" | custom-call | flops 3221225472 | bytes 3145728 | tf_op jit(solution)/shard_map/pallas_call | solution.py:354
  177.0 11.9 %shard_map.180 = (bf16[2,1024,192]{2,1,0:T(8,128)(2,1)}, f32[2,1024,3]{2,1,0:T(8,128)}) custom-call(s32[3]{0:T(128)} %pad_add_fusion.bits, s32[2]{0:T(128)} %dynamic-slice_reduce_fusion.lens, bf16[4,1024,384]{2,1,0:T(8,128)(2,1)} %get-tuple-element.53.qk, bf16[4,1024,192]{2,1,0:T(8,128)(2,1)} %get-tuple-element.54.v, ...), custom_call_target="tpu_custom_call" | custom-call | flops 3221225472 | bytes 3145728 | tf_op jit(solution)/shard_map/pallas_call | solution.py:354
  188.8 7.5 %shard_map.181 = (bf16[1024,768]{1,0:T(8,128)(2,1)}, f32[1024,768]{1,0:T(8,128)}, f32[1024,1]{1,0:T(8,128)}, bf16[768,1024]{1,0:T(8,128)(2,1)}) custom-call(bf16[1024,768]{1,0:T(8,128)(2,1)} %bitcast.266, bf16[2,1024,192]{2,1,0:T(8,128)(2,1)} %get-tuple-element.55.m0.mixed, bf16[2,1024,192]{2,1,0:T(8,128)(2,1)} %get-tuple-element.56.m1.mixed, ...), custom_call_target="tpu_custom_call" | custom-call | flops 1207959552 | bytes 9437184 | tf_op jit(solution)/shard_map/pallas_call | solution.py:537
  196.3 27.5 %shard_map.182 = (bf16[1024,768]{1,0:T(8,128)(2,1)}, f32[1024,768]{1,0:T(8,128)}, bf16[1024,768]{1,0:T(8,128)(2,1)}, bf16[768,1024]{1,0:T(8,128)(2,1)}, bf16[4,1...) custom-call(s32[3]{0:T(128)} %pad_add_fusion.bits, ...), custom_call_target="tpu_custom_call" | custom-call | flops 9663676416 | bytes 31457280 | tf_op jit(solution)/shard_map/pallas_call | solution.py:168
  223.9 19.8 %shard_map.183 = (bf16[2,2,2,2,96,768]{5,4,3,2,1,0:T(8,128)(2,1)}, bf16[2,2,2,2,96,768]{5,4,3,2,1,0:T(8,128)(2,1)}, f32[1024,768]{1,0:T(8,128)}) custom-call(s32[3]{0:T(128)} %pad_add_fusion.bits, bf16[768,1024]{1,0:T(8,128)(2,1)} %get-tuple-element.60.ht, bf16[768,1024]{1,0:T(8,128)(2,1)} %get-tuple-element.61.dt, ...), custom_call_target="tpu_custom_call" | custom-call | flops 9663676416 | bytes 23592960 | tf_op jit(solution)/shard_map/pallas_call | solution.py:281
  243.7 26.3 %shard_map.184 = (bf16[2,2,2,2,96,768]{5,4,3,2,1,0:T(8,128)(2,1)}, bf16[2,2,2,2,96,768]{5,4,3,2,1,0:T(8,128)(2,1)}, f32[1024,768]{1,0:T(8,128)}, bf16[1024,768]{...) custom-call(s32[3]{0:T(128)} %pad_add_fusion.bits, ...), custom_call_target="tpu_custom_call" | custom-call | flops 9663676416 | bytes 23592960 | tf_op jit(solution)/shard_map/pallas_call | solution.py:281
  270.9 19.8 %shard_map.186 = (bf16[2,1024,384]{2,1,0:T(8,128)(2,1)}, bf16[2,1024,192]{2,1,0:T(8,128)(2,1)}, bf16[2,2,2,2,3,32,512]{6,5,4,3,2,1,0:T(8,128)(2,1)}, bf16[2,2,2,2,3,32,512]{6,5,4,3,2,1,0:T(8,128)(2,1)}) custom-call(s32[3]{0:T(128)} %pad_add_fusion.bits, s32[2]{0:T(128)} %dynamic-slice_reduce_fusion.lens, bf16[4,1024,384]{2,1,0:T(8,128)(2,1)} %get-tuple-element.53.qk, ...), custom_call_target="tpu_custom_call" | custom-call | flops 8053063680 | bytes 5898240 | tf_op jit(solution)/shard_map/pallas_call | solution.py:442
  291.3 8.5 %shard_map.189 = (bf16[2,2,2,2,96,384]{5,4,3,2,1,0:T(8,128)(2,1)}, bf16[2,2,2,2,96,384]{5,4,3,2,1,0:T(8,128)(2,1)}) custom-call(s32[3]{0:T(128)} %pad_add_fusion.bits, bf16[768,1024]{1,0:T(8,128)(2,1)} %get-tuple-element.79.xt, bf16[768,1024]{1,0:T(8,128)(2,1)} %get-tuple-element.80.dat, bf16[2,1024,384]{2,1,0:T(8,128)(2,1)} %get-tuple-element.74.dqk1.dqk, ...), custom_call_target="tpu_custom_call" | custom-call | flops 2415919104 | bytes 6291456 | tf_op jit(solution)/shard_map/pallas_call | solution.py:565
  302.0 19.6 %shard_map.185 = (bf16[2,1024,384]{2,1,0:T(8,128)(2,1)}, bf16[2,1024,192]{2,1,0:T(8,128)(2,1)}, bf16[2,2,2,2,3,32,512]{6,5,4,3,2,1,0:T(8,128)(2,1)}, bf16[2,2,2,2,3,32,512]{6,5,4,3,2,1,0:T(8,128)(2,1)}) custom-call(s32[3]{0:T(128)} %pad_add_fusion.bits, s32[2]{0:T(128)} %dynamic-slice_reduce_fusion.lens, bf16[4,1024,384]{2,1,0:T(8,128)(2,1)} %get-tuple-element.53.qk, ...), custom_call_target="tpu_custom_call" | custom-call | flops 8053063680 | bytes 5898240 | tf_op jit(solution)/shard_map/pallas_call | solution.py:442
  322.2 8.3 %shard_map.188 = (bf16[2,2,2,2,96,384]{5,4,3,2,1,0:T(8,128)(2,1)}, bf16[2,2,2,2,96,384]{5,4,3,2,1,0:T(8,128)(2,1)}) custom-call(s32[3]{0:T(128)} %pad_add_fusion.bits, bf16[768,1024]{1,0:T(8,128)(2,1)} %get-tuple-element.79.xt, bf16[768,1024]{1,0:T(8,128)(2,1)} %get-tuple-element.80.dat, bf16[2,1024,384]{2,1,0:T(8,128)(2,1)} %get-tuple-element.72.dqk0.dqk, ...), custom_call_target="tpu_custom_call" | custom-call | flops 2415919104 | bytes 6291456 | tf_op jit(solution)/shard_map/pallas_call | solution.py:565
  330.5 4.0 collective-permute-start.44
  339.6 10.1 %shard_map.187 = f32[1024,768]{1,0:T(8,128)} custom-call(f32[1024,768]{1,0:T(8,128)} %get-tuple-element.69.dfirst, bf16[2,1024,384]{2,1,0:T(8,128)(2,1)} %get-tuple-element.72.dqk0.dqk, bf16[2,1024,384]{2,1,0:T(8,128)(2,1)} %get-tuple-element.74.dqk1.dqk, bf16[2,1024,192]{2,1,0:T(8,128)(2,1)} %get-tuple-element.75.dv0.dv, ...), custom_call_target="tpu_custom_call" | custom-call | flops 3623878656 | bytes 11010048 | tf_op jit(solution)/shard_map/pallas_call | solution.py:592
  356.5 5.8 %collective-permute-done.26 = bf16[2,2,96,384]{3,2,1,0:T(8,128)(2,1)S(1)} collective-permute-done((bf16[2,2,96,384]{3,2,1,0:T(8,128)(2,1)S(1)}, bf16[2,2,96,384]{3,2,1,0:T(8,128)(2,1)S(1)}, u32[]{:S(2)}, u32[]{:S(2)}) %collective-permute-start.26) | collective-permute-done | bytes 294944 | tf_op jit(solution)/shard_map/ppermute | solution.py:609
  369.4 5.2 %collective-permute-done.30 = bf16[2,2,96,384]{3,2,1,0:T(8,128)(2,1)S(1)} collective-permute-done((bf16[2,2,96,384]{3,2,1,0:T(8,128)(2,1)S(1)}, bf16[2,2,96,384]{3,2,1,0:T(8,128)(2,1)S(1)}, u32[]{:S(2)}, u32[]{:S(2)}) %collective-permute-start.30) | collective-permute-done | bytes 294944 | tf_op jit(solution)/shard_map/ppermute | solution.py:609
  375.1 6.0 %collective-permute-done.46 = bf16[2,2,2,3,32,512]{5,4,3,2,1,0:T(8,128)(2,1)S(1)} collective-permute-done((bf16[2,2,2,3,32,512]{5,4,3,2,1,0:T(8,128)(2,1)S(1)}, bf16[2,2,2,3,32,512]{5,4,3,2,1,0:T(8,128)(2,1)S(1)}, u32[]{:S(2)}, u32[]{:S(2)}) %collective-permute-start.46) | collective-permute-done | bytes 786464 | tf_op jit(solution)/shard_map/ppermute | solution.py:614
  390.7 6.9 %collective-permute-done.47 = bf16[2,2,3,32,512]{4,3,2,1,0:T(8,128)(2,1)S(1)} collective-permute-done((bf16[2,2,3,32,512]{4,3,2,1,0:T(8,128)(2,1)S(1)}, bf16[2,2,3,32,512]{4,3,2,1,0:T(8,128)(2,1)S(1)}, u32[]{:S(2)}, u32[]{:S(2)}) %collective-permute-start.47) | collective-permute-done | bytes 393248 | tf_op jit(solution)/shard_map/ppermute | solution.py:609
  397.8 13.7 %collective-permute-done.33 = bf16[2,2,2,96,768]{4,3,2,1,0:T(8,128)(2,1)S(1)} collective-permute-done((bf16[2,2,2,96,768]{4,3,2,1,0:T(8,128)(2,1)S(1)}, bf16[2,2,2,96,768]{4,3,2,1,0:T(8,128)(2,1)S(1)}, u32[]{:S(2)}, u32[]{:S(2)}) %collective-permute-start.33) | collective-permute-done | bytes 1179680 | tf_op jit(solution)/shard_map/ppermute | solution.py:614
  412.8 10.0 %collective-permute-done.36 = bf16[2,2,2,96,768]{4,3,2,1,0:T(8,128)(2,1)S(1)} collective-permute-done((bf16[2,2,2,96,768]{4,3,2,1,0:T(8,128)(2,1)S(1)}, bf16[2,2,2,96,768]{4,3,2,1,0:T(8,128)(2,1)S(1)}, u32[]{:S(2)}, u32[]{:S(2)}) %collective-permute-start.36) | collective-permute-done | bytes 1179680 | tf_op jit(solution)/shard_map/ppermute | solution.py:609
  425.5 8.0 %collective-permute-done.34 = bf16[2,2,96,768]{3,2,1,0:T(8,128)(2,1)S(1)} collective-permute-done((bf16[2,2,96,768]{3,2,1,0:T(8,128)(2,1)S(1)}, bf16[2,2,96,768]{3,2,1,0:T(8,128)(2,1)S(1)}, u32[]{:S(2)}, u32[]{:S(2)}) %collective-permute-start.34) | collective-permute-done | bytes 589856 | tf_op jit(solution)/shard_map/ppermute | solution.py:609
  441.9 11.0 %collective-permute-done.38 = bf16[2,2,96,768]{3,2,1,0:T(8,128)(2,1)} collective-permute-done((bf16[2,2,96,768]{3,2,1,0:T(8,128)(2,1)}, bf16[2,2,96,768]{3,2,1,0:T(8,128)(2,1)}, u32[]{:S(2)}, u32[]{:S(2)}) %collective-permute-start.38) | collective-permute-done | bytes 589856 | tf_op jit(solution)/shard_map/ppermute | solution.py:609
  456.1 9.2 %collective-permute-done.39 = bf16[2,96,768]{2,1,0:T(8,128)(2,1)S(1)} collective-permute-done((bf16[2,96,768]{2,1,0:T(8,128)(2,1)S(1)}, bf16[2,96,768]{2,1,0:T(8,128)(2,1)S(1)}, u32[]{:S(2)}, u32[]{:S(2)}) %collective-permute-start.39) | collective-permute-done | bytes 294944 | tf_op jit(solution)/shard_map/ppermute | solution.py:609
  (205 shorter events, 98.1 us)
Async XLA Ops:
  1.7 17.4 %collective-permute-start.16 = (bf16[2,96,768]{2,1,0:T(8,128)(2,1)S(1)}, bf16[2,96,768]{2,1,0:T(8,128)(2,1)S(1)}, u32[]{:S(2)}, u32[]{:S(2)}) collective-permute-start(bf16[2,96,768]{2,1,0:T(8,128)(2,1)S(1)} %get-tuple-element.141), channel_id=1, source_target_pairs={{0,16},{4,20},{8,24},{12,28},{16,0},{20,4},{24,8},{28,12},{1,17},{... | collective-permute-start | bytes 884744 | tf_op jit(solution)/shard_map/ppermute | solution.py:609
  19.2 17.7 %collective-permute-start.17 = (bf16[2,2,96,768]{3,2,1,0:T(8,128)(2,1)S(1)}, bf16[2,2,96,768]{3,2,1,0:T(8,128)(2,1)S(1)}, u32[]{:S(2)}, u32[]{:S(2)}) collective-permute-start(bf16[2,2,96,768]{3,2,1,0:T(8,128)(2,1)S(1)} %get-tuple-element.124), channel_id=1, source_target_pairs={{0,8},{4,12},{8,0},{12,4},{16,24},{20,28},{24,16},{28,20},{1,9},{5... | collective-permute-start | bytes 1769480 | tf_op jit(solution)/shard_map/ppermute | solution.py:609
  20.0 21.0 %collective-permute-start = (bf16[2,96,384]{2,1,0:T(8,128)(2,1)S(1)}, bf16[2,96,384]{2,1,0:T(8,128)(2,1)S(1)}, u32[]{:S(2)}, u32[]{:S(2)}) collective-permute-start(bf16[2,96,384]{2,1,0:T(8,128)(2,1)S(1)} %get-tuple-element.153), channel_id=1, source_target_pairs={{0,16},{4,20},{8,24},{12,28},{16,0},{20,4},{24,8},{28,12},{1,17},{... | collective-permute-start | bytes 442376 | tf_op jit(solution)/shard_map/ppermute | solution.py:609
  53.4 66.3 %collective-permute-start.22 = (bf16[2,2,2,96,768]{4,3,2,1,0:T(8,128)(2,1)S(1)}, bf16[2,2,2,96,768]{4,3,2,1,0:T(8,128)(2,1)S(1)}, u32[]{:S(2)}, u32[]{:S(2)}) collective-permute-start(bf16[2,2,2,96,768]{4,3,2,1,0:T(8,128)(2,1)S(1)} %get-tuple-element.107), channel_id=1, source_target_pairs={{0,4},{4,0},{8,12},{12,8},{16,20},{20,16},{24,28},{28,24},{1,5},{5... | collective-permute-start | bytes 3538952 | tf_op jit(solution)/shard_map/ppermute | solution.py:609
  60.9 43.4 %collective-permute-start.6 = (bf16[2,2,2,96,384]{4,3,2,1,0:T(8,128)(2,1)S(1)}, bf16[2,2,2,96,384]{4,3,2,1,0:T(8,128)(2,1)S(1)}, u32[]{:S(2)}, u32[]{:S(2)}) collective-permute-start(bf16[2,2,2,96,384]{4,3,2,1,0:T(8,128)(2,1)S(1)} %get-tuple-element.127), channel_id=1, source_target_pairs={{0,4},{4,0},{8,12},{12,8},{16,20},{20,16},{24,28},{28,24},{1,5},{5... | collective-permute-start | bytes 1769480 | tf_op jit(solution)/shard_map/ppermute | solution.py:609
  66.5 55.0 %collective-permute-start.19 = (bf16[2,2,2,96,768]{4,3,2,1,0:T(8,128)(2,1)S(1)}, bf16[2,2,2,96,768]{4,3,2,1,0:T(8,128)(2,1)S(1)}, u32[]{:S(2)}, u32[]{:S(2)}) collective-permute-start(bf16[2,2,2,96,768]{4,3,2,1,0:T(8,128)(2,1)S(1)} %get-tuple-element.111), channel_id=1, source_target_pairs={{0,2},{1,3},{2,0},{3,1},{4,6},{5,7},{6,4},{7,5},{8,10},{9,11},{10,... | collective-permute-start | bytes 3538952 | tf_op jit(solution)/shard_map/ppermute | solution.py:614
  67.1 43.5 %collective-permute-start.2 = (bf16[2,2,96,384]{3,2,1,0:T(8,128)(2,1)S(1)}, bf16[2,2,96,384]{3,2,1,0:T(8,128)(2,1)S(1)}, u32[]{:S(2)}, u32[]{:S(2)}) collective-permute-start(bf16[2,2,96,384]{3,2,1,0:T(8,128)(2,1)S(1)} %bitcast.267), channel_id=1, source_target_pairs={{0,4},{4,0},{8,12},{12,8},{16,20},{20,16},{24,28},{28,24},{1,5},{5... | collective-permute-start | bytes 884744 | tf_op jit(solution)/shard_map/ppermute | solution.py:609
  72.3 46.8 %collective-permute-start.10 = (bf16[2,2,3,32,512]{4,3,2,1,0:T(8,128)(2,1)S(1)}, bf16[2,2,3,32,512]{4,3,2,1,0:T(8,128)(2,1)S(1)}, u32[]{:S(2)}, u32[]{:S(2)}) collective-permute-start(bf16[2,2,3,32,512]{4,3,2,1,0:T(8,128)(2,1)S(1)} %bitcast.263), channel_id=1, source_target_pairs={{0,4},{4,0},{8,12},{12,8},{16,20},{20,16},{24,28},{28,24},{1,5},{5... | collective-permute-start | bytes 1179656 | tf_op jit(solution)/shard_map/ppermute | solution.py:609
  104.3 32.2 %collective-permute-start.13 = (bf16[2,2,2,3,32,512]{5,4,3,2,1,0:T(8,128)(2,1)S(1)}, bf16[2,2,2,3,32,512]{5,4,3,2,1,0:T(8,128)(2,1)S(1)}, u32[]{:S(2)}, u32[]{:S(2)}) collective-permute-start(bf16[2,2,2,3,32,512]{5,4,3,2,1,0:T(8,128)(2,1)S(1)} %get-tuple-element.115), channel_id=1, source_target_pairs={{0,4},{4,0},{8,12},{12,8},{16,20},{20,16},{24,28},{28,24},{1,5},{5... | collective-permute-start | bytes 2359304 | tf_op jit(solution)/shard_map/ppermute | solution.py:609
  110.6 38.6 %collective-permute-start.7 = (bf16[2,2,2,2,96,384]{5,4,3,2,1,0:T(8,128)(2,1)S(1)}, bf16[2,2,2,2,96,384]{5,4,3,2,1,0:T(8,128)(2,1)S(1)}, u32[]{:S(2)}, u32[]{:S(2)}) collective-permute-start(bf16[2,2,2,2,96,384]{5,4,3,2,1,0:T(8,128)(2,1)S(1)} %pad_maximum_fusion.5.wb0), channel_id=1, source_target_pairs={{0,1},{1,0},{2,3},{3,2},{4,5},{5,4},{6,7},{7,6},{8,9},{9,8},{10,11... | collective-permute-start | bytes 3538952 | tf_op jit(solution)/shard_map/ppermute | solution.py:614
  119.7 28.2 %collective-permute-start.11 = (bf16[2,2,2,3,32,512]{5,4,3,2,1,0:T(8,128)(2,1)S(1)}, bf16[2,2,2,3,32,512]{5,4,3,2,1,0:T(8,128)(2,1)S(1)}, u32[]{:S(2)}, u32[]{:S(2)}) collective-permute-start(bf16[2,2,2,3,32,512]{5,4,3,2,1,0:T(8,128)(2,1)S(1)} %get-tuple-element.119), channel_id=1, source_target_pairs={{0,2},{1,3},{2,0},{3,1},{4,6},{5,7},{6,4},{7,5},{8,10},{9,11},{10,... | collective-permute-start | bytes 2359304 | tf_op jit(solution)/shard_map/ppermute | solution.py:614
  121.5 74.8 %collective-permute-start.23 = (bf16[2,2,2,2,96,768]{5,4,3,2,1,0:T(8,128)(2,1)S(1)}, bf16[2,2,2,2,96,768]{5,4,3,2,1,0:T(8,128)(2,1)}, u32[]{:S(2)}, u32[]{:S(2)}) collective-permute-start(bf16[2,2,2,2,96,768]{5,4,3,2,1,0:T(8,128)(2,1)S(1)} %pad_maximum_fusion.1.db0.db), channel_id=1, source_target_pairs={{0,1},{1,0},{2,3},{3,2},{4,5},{5,4},{6,7},{7,6},{8,9},{9,8},{10,11... | collective-permute-start | bytes 7077896 | tf_op jit(solution)/shard_map/ppermute | solution.py:614
  135.3 61.0 %collective-permute-start.20 = (bf16[2,2,2,2,96,768]{5,4,3,2,1,0:T(8,128)(2,1)}, bf16[2,2,2,2,96,768]{5,4,3,2,1,0:T(8,128)(2,1)}, u32[]{:S(2)}, u32[]{:S(2)}) collective-permute-start(bf16[2,2,2,2,96,768]{5,4,3,2,1,0:T(8,128)(2,1)} %pad_maximum_fusion.ua0.ua), channel_id=1, source_target_pairs={{0,1},{1,0},{2,3},{3,2},{4,5},{5,4},{6,7},{7,6},{8,9},{9,8},{10,11... | collective-permute-start | bytes 7077896 | tf_op jit(solution)/shard_map/ppermute | solution.py:614
  148.0 29.0 %collective-permute-start.15 = (bf16[2,2,2,2,3,32,512]{6,5,4,3,2,1,0:T(8,128)(2,1)}, bf16[2,2,2,2,3,32,512]{6,5,4,3,2,1,0:T(8,128)(2,1)}, u32[]{:S(2)}, u32[]{:S(2)}) collective-permute-start(bf16[2,2,2,2,3,32,512]{6,5,4,3,2,1,0:T(8,128)(2,1)} %pad_maximum_fusion.3.gb), channel_id=1, source_target_pairs={{0,1},{1,0},{2,3},{3,2},{4,5},{5,4},{6,7},{7,6},{8,9},{9,8},{10,11... | collective-permute-start | bytes 4718600 | tf_op jit(solution)/shard_map/ppermute | solution.py:614
  150.3 26.7 %collective-permute-start.14 = (bf16[2,2,2,2,3,32,512]{6,5,4,3,2,1,0:T(8,128)(2,1)}, bf16[2,2,2,2,3,32,512]{6,5,4,3,2,1,0:T(8,128)(2,1)}, u32[]{:S(2)}, u32[]{:S(2)}) collective-permute-start(bf16[2,2,2,2,3,32,512]{6,5,4,3,2,1,0:T(8,128)(2,1)} %pad_maximum_fusion.2.ga), channel_id=1, source_target_pairs={{0,1},{1,0},{2,3},{3,2},{4,5},{5,4},{6,7},{7,6},{8,9},{9,8},{10,11... | collective-permute-start | bytes 4718600 | tf_op jit(solution)/shard_map/ppermute | solution.py:614
  270.8 19.9 %collective-permute-start.40 = (f32[4,768]{1,0:T(4,128)S(1)}, f32[4,768]{1,0:T(4,128)S(1)}, u32[]{:S(2)}, u32[]{:S(2)}) collective-permute-start(f32[4,768]{1,0:T(4,128)S(1)} %pad_maximum_fusion.28), channel_id=1, source_target_pairs={{0,1},{1,0},{2,3},{3,2},{4,5},{5,4},{6,7},{7,6},{8,9},{9,8},{10,11... | collective-permute-start | bytes 36872 | tf_op jit(solution)/shard_map/ppermute | solution.py:690
  299.8 34.7 %collective-permute-start.24 = (bf16[2,2,2,2,96,384]{5,4,3,2,1,0:T(8,128)(2,1)}, bf16[2,2,2,2,96,384]{5,4,3,2,1,0:T(8,128)(2,1)S(1)}, u32[]{:S(2)}, u32[]{:S(2)}) collective-permute-start(bf16[2,2,2,2,96,384]{5,4,3,2,1,0:T(8,128)(2,1)} %get-tuple-element.82), channel_id=1, source_target_pairs={{0,1},{1,0},{2,3},{3,2},{4,5},{5,4},{6,7},{7,6},{8,9},{9,8},{10,11... | collective-permute-start | bytes 3538952 | tf_op jit(solution)/shard_map/ppermute | solution.py:614
  300.2 37.9 %collective-permute-start.27 = (bf16[2,2,2,2,96,384]{5,4,3,2,1,0:T(8,128)(2,1)}, bf16[2,2,2,2,96,384]{5,4,3,2,1,0:T(8,128)(2,1)S(1)}, u32[]{:S(2)}, u32[]{:S(2)}) collective-permute-start(bf16[2,2,2,2,96,384]{5,4,3,2,1,0:T(8,128)(2,1)} %get-tuple-element.84), channel_id=1, source_target_pairs={{0,1},{1,0},{2,3},{3,2},{4,5},{5,4},{6,7},{7,6},{8,9},{9,8},{10,11... | collective-permute-start | bytes 3538952 | tf_op jit(solution)/shard_map/ppermute | solution.py:614
  300.4 21.8 %collective-permute-start.42 = (f32[4,768]{1,0:T(4,128)S(1)}, f32[4,768]{1,0:T(4,128)S(1)}, u32[]{:S(2)}, u32[]{:S(2)}) collective-permute-start(f32[4,768]{1,0:T(4,128)S(1)} %fusion.64), channel_id=1, source_target_pairs={{0,4},{4,0},{8,12},{12,8},{16,20},{20,16},{24,28},{28,24},{1,5},{5... | collective-permute-start | bytes 36872 | tf_op jit(solution)/shard_map/ppermute | solution.py:690
  321.6 33.9 %collective-permute-start.45 = (bf16[2,2,2,2,3,32,512]{6,5,4,3,2,1,0:T(8,128)(2,1)}, bf16[2,2,2,2,3,32,512]{6,5,4,3,2,1,0:T(8,128)(2,1)S(1)}, u32[]{:S(2)}, u32[]{:S(2)}) collective-permute-start(bf16[2,2,2,2,3,32,512]{6,5,4,3,2,1,0:T(8,128)(2,1)} %get-tuple-element.94), channel_id=1, source_target_pairs={{0,1},{1,0},{2,3},{3,2},{4,5},{5,4},{6,7},{7,6},{8,9},{9,8},{10,11... | collective-permute-start | bytes 4718600 | tf_op jit(solution)/shard_map/ppermute | solution.py:614
  321.7 46.6 %collective-permute-start.48 = (bf16[2,2,2,2,3,32,512]{6,5,4,3,2,1,0:T(8,128)(2,1)}, bf16[2,2,2,2,3,32,512]{6,5,4,3,2,1,0:T(8,128)(2,1)S(1)}, u32[]{:S(2)}, u32[]{:S(2)}) collective-permute-start(bf16[2,2,2,2,3,32,512]{6,5,4,3,2,1,0:T(8,128)(2,1)} %get-tuple-element.96), channel_id=1, source_target_pairs={{0,1},{1,0},{2,3},{3,2},{4,5},{5,4},{6,7},{7,6},{8,9},{9,8},{10,11... | collective-permute-start | bytes 4718600 | tf_op jit(solution)/shard_map/ppermute | solution.py:614
  330.5 19.2 %collective-permute-start.44 = (f32[4,768]{1,0:T(4,128)S(1)}, f32[4,768]{1,0:T(4,128)S(1)}, u32[]{:S(2)}, u32[]{:S(2)}) collective-permute-start(f32[4,768]{1,0:T(4,128)S(1)} %add.365), channel_id=1, source_target_pairs={{0,16},{4,20},{8,24},{12,28},{16,0},{20,4},{24,8},{28,12},{1,17},{... | collective-permute-start | bytes 36872 | tf_op jit(solution)/shard_map/ppermute | solution.py:690
  349.7 32.6 %collective-permute-start.32 = (bf16[2,2,2,2,96,768]{5,4,3,2,1,0:T(8,128)(2,1)}, bf16[2,2,2,2,96,768]{5,4,3,2,1,0:T(8,128)(2,1)S(1)}, u32[]{:S(2)}, u32[]{:S(2)}) collective-permute-start(bf16[2,2,2,2,96,768]{5,4,3,2,1,0:T(8,128)(2,1)} %get-tuple-element.86), channel_id=1, source_target_pairs={{0,1},{1,0},{2,3},{3,2},{4,5},{5,4},{6,7},{7,6},{8,9},{9,8},{10,11... | collective-permute-start | bytes 7077896 | tf_op jit(solution)/shard_map/ppermute | solution.py:614
  351.7 32.5 %collective-permute-start.35 = (bf16[2,2,2,2,96,768]{5,4,3,2,1,0:T(8,128)(2,1)}, bf16[2,2,2,2,96,768]{5,4,3,2,1,0:T(8,128)(2,1)S(1)}, u32[]{:S(2)}, u32[]{:S(2)}) collective-permute-start(bf16[2,2,2,2,96,768]{5,4,3,2,1,0:T(8,128)(2,1)} %get-tuple-element.88), channel_id=1, source_target_pairs={{0,1},{1,0},{2,3},{3,2},{4,5},{5,4},{6,7},{7,6},{8,9},{9,8},{10,11... | collective-permute-start | bytes 7077896 | tf_op jit(solution)/shard_map/ppermute | solution.py:614
  362.3 18.8 %collective-permute-start.46 = (bf16[2,2,2,3,32,512]{5,4,3,2,1,0:T(8,128)(2,1)S(1)}, bf16[2,2,2,3,32,512]{5,4,3,2,1,0:T(8,128)(2,1)S(1)}, u32[]{:S(2)}, u32[]{:S(2)}) collective-permute-start(bf16[2,2,2,3,32,512]{5,4,3,2,1,0:T(8,128)(2,1)S(1)} %fusion.6), channel_id=1, source_target_pairs={{0,2},{1,3},{2,0},{3,1},{4,6},{5,7},{6,4},{7,5},{8,10},{9,11},{10,... | collective-permute-start | bytes 2359304 | tf_op jit(solution)/shard_map/ppermute | solution.py:614
  368.6 20.5 %collective-permute-start.49 = (bf16[2,2,2,3,32,512]{5,4,3,2,1,0:T(8,128)(2,1)S(1)}, bf16[2,2,2,3,32,512]{5,4,3,2,1,0:T(8,128)(2,1)S(1)}, u32[]{:S(2)}, u32[]{:S(2)}) collective-permute-start(bf16[2,2,2,3,32,512]{5,4,3,2,1,0:T(8,128)(2,1)S(1)} %fusion.7), channel_id=1, source_target_pairs={{0,4},{4,0},{8,12},{12,8},{16,20},{20,16},{24,28},{28,24},{1,5},{5... | collective-permute-start | bytes 2359304 | tf_op jit(solution)/shard_map/ppermute | solution.py:609
  381.2 16.4 %collective-permute-start.47 = (bf16[2,2,3,32,512]{4,3,2,1,0:T(8,128)(2,1)S(1)}, bf16[2,2,3,32,512]{4,3,2,1,0:T(8,128)(2,1)S(1)}, u32[]{:S(2)}, u32[]{:S(2)}) collective-permute-start(bf16[2,2,3,32,512]{4,3,2,1,0:T(8,128)(2,1)S(1)} %fusion.10), channel_id=1, source_target_pairs={{0,4},{4,0},{8,12},{12,8},{16,20},{20,16},{24,28},{28,24},{1,5},{5... | collective-permute-start | bytes 1179656 | tf_op jit(solution)/shard_map/ppermute | solution.py:609
  382.6 29.0 %collective-permute-start.33 = (bf16[2,2,2,96,768]{4,3,2,1,0:T(8,128)(2,1)S(1)}, bf16[2,2,2,96,768]{4,3,2,1,0:T(8,128)(2,1)S(1)}, u32[]{:S(2)}, u32[]{:S(2)}) collective-permute-start(bf16[2,2,2,96,768]{4,3,2,1,0:T(8,128)(2,1)S(1)} %fusion), channel_id=1, source_target_pairs={{0,2},{1,3},{2,0},{3,1},{4,6},{5,7},{6,4},{7,5},{8,10},{9,11},{10,... | collective-permute-start | bytes 3538952 | tf_op jit(solution)/shard_map/ppermute | solution.py:614
  384.4 38.4 %collective-permute-start.36 = (bf16[2,2,2,96,768]{4,3,2,1,0:T(8,128)(2,1)S(1)}, bf16[2,2,2,96,768]{4,3,2,1,0:T(8,128)(2,1)S(1)}, u32[]{:S(2)}, u32[]{:S(2)}) collective-permute-start(bf16[2,2,2,96,768]{4,3,2,1,0:T(8,128)(2,1)S(1)} %fusion.1), channel_id=1, source_target_pairs={{0,4},{4,0},{8,12},{12,8},{16,20},{20,16},{24,28},{28,24},{1,5},{5... | collective-permute-start | bytes 3538952 | tf_op jit(solution)/shard_map/ppermute | solution.py:609
  389.3 34.4 %collective-permute-start.50 = (bf16[2,2,3,32,512]{4,3,2,1,0:T(8,128)(2,1)S(1)}, bf16[2,2,3,32,512]{4,3,2,1,0:T(8,128)(2,1)S(1)}, u32[]{:S(2)}, u32[]{:S(2)}) collective-permute-start(bf16[2,2,3,32,512]{4,3,2,1,0:T(8,128)(2,1)S(1)} %fusion.8), channel_id=1, source_target_pairs={{0,2},{1,3},{2,0},{3,1},{4,6},{5,7},{6,4},{7,5},{8,10},{9,11},{10,... | collective-permute-start | bytes 1179656 | tf_op jit(solution)/shard_map/ppermute | solution.py:614
  411.8 21.7 %collective-permute-start.34 = (bf16[2,2,96,768]{3,2,1,0:T(8,128)(2,1)S(1)}, bf16[2,2,96,768]{3,2,1,0:T(8,128)(2,1)S(1)}, u32[]{:S(2)}, u32[]{:S(2)}) collective-permute-start(bf16[2,2,96,768]{3,2,1,0:T(8,128)(2,1)S(1)} %fusion.4), channel_id=1, source_target_pairs={{0,4},{4,0},{8,12},{12,8},{16,20},{20,16},{24,28},{28,24},{1,5},{5... | collective-permute-start | bytes 1769480 | tf_op jit(solution)/shard_map/ppermute | solution.py:609
  435.6 17.3 %collective-permute-start.38 = (bf16[2,2,96,768]{3,2,1,0:T(8,128)(2,1)}, bf16[2,2,96,768]{3,2,1,0:T(8,128)(2,1)}, u32[]{:S(2)}, u32[]{:S(2)}) collective-permute-start(bf16[2,2,96,768]{3,2,1,0:T(8,128)(2,1)} %pad_maximum_fusion.14), channel_id=1, source_target_pairs={{0,8},{4,12},{8,0},{12,4},{16,24},{20,28},{24,16},{28,20},{1,9},{5... | collective-permute-start | bytes 1769480 | tf_op jit(solution)/shard_map/ppermute | solution.py:609
  (42 other events, 615.4 us)
